TPU v7x, 32 devices: a whole 2x2x4 slice. The times are simulated.
32 devices in a mesh: expert: 16 (over z, y, x), loop: 2 (over core).
Axes of the slice: x: 2, y: 2, z: 4, core: 2. Of those that a mesh axis runs over, the one named last changes fastest.
Arguments:
- tokens: bfloat16 [2048, 7168], P('expert', 'loop'), may hold values from -6 to 6
- expert_ids: int32 [2048, 8], P('expert'), may hold values from 0 to 255, all different within a row; in each aligned block of 128 rows (0 to 127, 128 to 255, ...) at most 8 rows name the same one
- route_weights: float32 [2048, 8], P('expert'), may hold values from 0.1 to 1
- up_proj: bfloat16 [16, 7168, 1024], P('expert', None, 'loop'), may hold values from -0.0625 to 0.0625
- down_proj: bfloat16 [16, 1024, 7168], P('expert', None, 'loop'), may hold values from -0.1875 to 0.1875
Outputs:
- combined: bfloat16 [2048, 7168], P('expert', 'loop')
Inputs may be any that keep to these rules, and one draw needn't show every extreme that they name: `expert_ids`: each row names 8 different experts. Among the 128 rows held by one device along `expert`, no expert is chosen by more than 8 rows, a bound that some block reaches.
All inputs are finite; a program needn't handle non-finite values.
Results may differ from a plain program's by a relative error of at most 0.0058.
Values may be sent and summed in bfloat16 or wider, within the bound.
No kernel may reach another device: no remote copies, remote signals or barrier semaphores. Data moves between devices by JAX's collectives and lax.ppermute only.
A program may use at most 64 MiB of HBM per device.

v0:
```python
import jax
import jax.numpy as jnp
from jax import lax
from jax.sharding import PartitionSpec as P


def slot_tables(expert_ids, route_weights, flight, capacity):
    tok_count = expert_ids.shape[0]
    experts = jnp.arange(flight, dtype=jnp.int32)
    matches = expert_ids[:, :, None] == experts[None, None, :]
    chosen = jnp.any(matches, axis=1)
    weight = jnp.sum(jnp.where(matches, route_weights[:, :, None], 0.0), axis=1)
    ranking = jnp.cumsum(chosen.astype(jnp.int32), axis=0) - 1
    places = jnp.arange(capacity, dtype=jnp.int32)
    picked = chosen[:, :, None] & (ranking[:, :, None] == places[None, None, :])
    tok_index = jnp.arange(tok_count, dtype=jnp.int32)
    slot_token = jnp.sum(jnp.where(picked, tok_index[:, None, None], 0), axis=0).reshape(
        flight * capacity
    )
    slot_weight = jnp.sum(jnp.where(picked, weight[:, :, None], 0.0), axis=0).reshape(
        flight * capacity
    )
    slot_live = jnp.any(picked, axis=0).reshape(flight * capacity)
    return (slot_token, slot_weight, slot_live)


def on_device(tokens, expert_ids, route_weights, up_proj, down_proj):
    tok_rows = tokens.shape[0]
    capacity = tok_rows // 16
    owners = lax.axis_size("expert")
    per_owner = up_proj.shape[0]
    flight = owners * per_owner
    slot_count = owners * capacity
    slot_token, slot_weight, slot_live = slot_tables(expert_ids, route_weights, flight, capacity)
    live_mask = slot_live.astype(jnp.bfloat16)[:, None]
    features = lax.all_gather(tokens, "loop", axis=1, tiled=True)
    full_width = features.shape[1]
    outgoing = (jnp.take(features, slot_token, axis=0) * live_mask).reshape(
        owners, per_owner * capacity, full_width
    )
    arrived = lax.all_to_all(outgoing, "expert", split_axis=0, concat_axis=0, tiled=True)
    slot_rows = (
        arrived.reshape(owners, per_owner, capacity, full_width)
        .transpose(1, 0, 2, 3)
        .reshape(per_owner, slot_count, full_width)
    )
    up_sums = jnp.einsum("esd,edh->esh", slot_rows, up_proj, preferred_element_type=jnp.float32)
    hidden = jax.nn.silu(up_sums).astype(jnp.bfloat16)
    out_width = down_proj.shape[2]
    out_rows = jnp.einsum(
        "esh,ehd->esd",
        lax.all_gather(hidden, "loop", axis=2, tiled=True),
        down_proj,
        preferred_element_type=jnp.float32,
    ).astype(jnp.bfloat16)
    homeward = (
        out_rows.reshape(per_owner, owners, capacity, out_width)
        .transpose(1, 0, 2, 3)
        .reshape(owners, per_owner * capacity, out_width)
    )
    returned = lax.all_to_all(homeward, "expert", split_axis=0, concat_axis=0, tiled=True).reshape(
        flight * capacity, out_width
    )
    scaled = slot_weight[:, None] * returned.astype(jnp.float32)
    combined = jax.ops.segment_sum(scaled, slot_token, num_segments=tok_rows)
    return combined.astype(jnp.bfloat16)


def solution(mesh):
    return jax.shard_map(
        on_device,
        mesh=mesh,
        in_specs=(
            P("expert", "loop"),
            P("expert", None),
            P("expert", None),
            P("expert", None, "loop"),
            P("expert", None, "loop"),
        ),
        out_specs=P("expert", "loop"),
        check_vma=False,
    )
```

profile of v0, /device:TPU:0, one launch (start us, length us, event | category | flops | bytes accessed | tf_op | source)
XLA Modules:
  0.0 124.3 jit_solution(4287521138012820241)
XLA Ops:
  6.5 0.0 all-gather.3.cloned.1.call-start
  6.5 0.7 all-gather.3.cloned.1.call-update
  7.3 0.7 fusion.20
  8.0 0.1 copy.10
  8.1 0.2 reduce_window_sum.11
  8.3 0.1 copy.11
  8.3 0.4 select_reduce_fusion.2
  8.7 0.1 broadcast_in_dim_reshape.4
  8.8 0.4 fusion.22
  9.2 12.6 %all-gather.3.cloned.1.call-done = bf16[128,7168]{1,0:T(8,128)(2,1)} async-done(((bf16[128,3584]{1,0:T(8,128)(2,1)}), bf16[128,7168]{1,0:T(8,128)(2,1)}) %all-gather.3.cloned.1.call-update) | async-done | bytes 1835024 | tf_op jit(solution)/shard_map/all_gather | solution.py:36
  21.8 5.1 %gather_fusion = bf16[128,7168]{1,0:T(8,128)(2,1)S(1)} fusion(bf16[128,7168]{1,0:T(8,128)(2,1)} %all-gather.3.cloned.1.call-done, s32[1024]{0:T(1024)S(1)} %pad_clamp_fusion), kind=kCustom, calls=%fused_computation | custom fusion | bytes 3670528 | tf_op jit(solution)/shard_map/jit(_take)/gather | solution.py:38
  26.9 0.2 fusion.12
  27.2 0.0 slice-start
  27.2 51.1 %all_to_all.10 = bf16[16,8,7168]{2,1,0:T(8,128)(2,1)S(1)} all-to-all(bf16[16,8,7168]{2,1,0:T(8,128)(2,1)S(1)} %fusion.12), channel_id=1, replica_groups=mesh['expert'=16,'loop'=2] {'expert'}, dimensions={0} | all-to-all | bytes 3670016 | tf_op jit(solution)/shard_map/all_to_all | solution.py:41
  78.3 0.0 slice-start.1
  78.3 4.4 %multiply_convert_fusion = bf16[128,512]{1,0:T(8,128)(2,1)S(1)} fusion(bf16[1,7168,512]{2,1,0:T(8,128)(2,1)} %param.8, bf16[16,8,7168]{2,1,0:T(8,128)(2,1)S(1)} %all_to_all.10), kind=kOutput, calls=%fused_computation.16 | convolution fusion | flops 939851776 | bytes 9306112 | tf_op jit(solution)/shard_map/esd,edh->esh/dot_general | solution.py:47
  82.7 2.0 %all-gather = bf16[128,1024]{1,0:T(8,128)(2,1)S(1)} all-gather(bf16[128,512]{1,0:T(8,128)(2,1)S(1)} %multiply_convert_fusion), channel_id=2, replica_groups=mesh['expert'=16,'loop'=2] {'loop'}, dimensions={1}, use_global_device_ids=true | all-gather | bytes 393216 | tf_op jit(solution)/shard_map/all_gather | solution.py:52
  84.7 0.0 slice-done
  84.7 0.0 slice-done.1
  84.7 2.1 %fusion.7 = bf16[16,8,3584]{2,1,0:T(8,128)(2,1)} fusion(bf16[128,1024]{1,0:T(8,128)(2,1)S(1)} %all-gather, bf16[1,1024,3584]{2,1,0:T(8,128)(2,1)S(1)} %bitcast.33), kind=kOutput, calls=%fused_computation.7 | convolution fusion | flops 939982848 | bytes 8519680 | tf_op jit(solution)/shard_map/esh,ehd->esd/dot_general | solution.py:50
  86.7 0.0 copy-start
  86.7 0.0 copy-start.1
  86.7 3.8 %all-to-all-start.1 = ((bf16[16,8,3584]{2,1,0:T(8,128)(2,1)}), bf16[16,8,3584]{2,1,0:T(8,128)(2,1)S(1)}, u32[]{:S(2)}, u32[]{:S(2)}) async-start(bf16[16,8,3584]{2,1,0:T(8,128)(2,1)} %fusion.7), calls=%async_computation.1 | async-start | bytes 1835008 | tf_op jit(solution)/shard_map/all_to_all | solution.py:61
  90.5 0.1 reshape.106
  90.6 0.0 copy-done
  90.6 0.0 copy-done.1
  90.6 0.1 select_reduce_fusion
  90.7 0.1 mul.24
  90.8 22.0 %all-to-all-done.1 = bf16[16,8,3584]{2,1,0:T(8,128)(2,1)S(1)} async-done(((bf16[16,8,3584]{2,1,0:T(8,128)(2,1)}), bf16[16,8,3584]{2,1,0:T(8,128)(2,1)S(1)}, u32[]{:S(2)}, u32[]{:S(2)}) %all-to-all-start.1) | async-done | bytes 917536 | tf_op jit(solution)/shard_map/all_to_all | solution.py:61
  112.8 3.6 %scatter_custom_fusion = f32[128,3584]{1,0:T(8,128)S(1)} fusion(s32[128]{0:T(128)S(1)} %reshape.106, bf16[16,8,3584]{2,1,0:T(8,128)(2,1)S(1)} %all-to-all-done.1, f32[128]{0:T(128)S(1)} %mul.24, f32[]{:T(128)} %constant.11.clone.1), kind=kCustom, calls=%fused_computation.9 | custom fusion | flops 1376256 | bytes 2753028 | tf_op jit(solution)/shard_map/scatter-add | solution.py:65
  116.4 1.0 convert_element_type.40
  (8 shorter events, 0.1 us)
Async XLA Ops:
  6.5 15.3 %all-gather.3.cloned.1.call-start = ((), (), s32[]{:S(2)}) async-start(), calls=%async_computation.2 | async-start | bytes 2752512 | tf_op jit(solution)/shard_map/all_gather | solution.py:36
  27.2 57.5 %slice-start = ((s8[7340032]{0:T(1024)(128)(4,1)}), s8[4194304]{0:T(1024)(128)(4,1)S(1)}, s32[]{:S(2)}) async-start(s8[7340032]{0:T(1024)(128)(4,1)} %bitcast.32), calls=%async_computation.3 | async-start | bytes 8388608
  78.3 6.4 %slice-start.1 = ((s8[7340032]{0:T(1024)(128)(4,1)}), s8[3145728]{0:T(1024)(128)(4,1)S(1)}, s32[]{:S(2)}) async-start(s8[7340032]{0:T(1024)(128)(4,1)} %bitcast.32), calls=%async_computation.4 | async-start | bytes 6291456
  86.7 3.9 %copy-start = (s32[128,8]{0,1:T(8,128)S(1)}, s32[128,8]{0,1:T(8,128)}, u32[]{:S(2)}) copy-start(s32[128,8]{0,1:T(8,128)} %param.6) | copy-start | bytes 12292
  86.7 3.9 %copy-start.1 = (f32[128,8]{0,1:T(8,128)S(1)}, f32[128,8]{0,1:T(8,128)}, u32[]{:S(2)}) copy-start(f32[128,8]{0,1:T(8,128)} %param.7) | copy-start | bytes 12292
  86.7 26.1 %all-to-all-start.1 = ((bf16[16,8,3584]{2,1,0:T(8,128)(2,1)}), bf16[16,8,3584]{2,1,0:T(8,128)(2,1)S(1)}, u32[]{:S(2)}, u32[]{:S(2)}) async-start(bf16[16,8,3584]{2,1,0:T(8,128)(2,1)} %fusion.7), calls=%async_computation.1 | async-start | bytes 1835008 | tf_op jit(solution)/shard_map/all_to_all | solution.py:61
Sparse Core Ops, SparseCore 0:
  8.9 12.8 all-gather.2
where the time goes:
time: 125 us; the launch traced here: 124 us
  blocking collectives  53.1 us (42%)
  waiting for transfers between devices  35.3 us (28%)
  between operations  13.5 us (11%)
  other arithmetic  6.58 us (5%)
  matrix products  6.47 us (5%)
  local copies, waits for them, and re-layouts  5.53 us (4%)
  starting transfers between devices  3.77 us (3%)
    all_to_all x1, blocking collectives, on_device(): lax.all_to_all(outgoing, 'expert', split_axis=0, concat_axis=0, tiled=True)  51.1 us
    all_to_all x1, waiting for transfers between devices, on_device(): lax.all_to_all(homeward, 'expert', split_axis=0, concat_axis=0, tiled=True)  22 us
    all_gather x1, waiting for transfers between devices, on_device(): features = lax.all_gather(tokens, 'loop', axis=1, tiled=True)  12.6 us
    gather x1, local copies, waits for them, and re-layouts, on_device(): jnp.take(features, slot_token, axis=0) * live_mask  5.1 us
    dot_general x1, matrix products, on_device(): jnp.einsum('esd,edh->esh', slot_rows, up_proj, preferred_element_type=jnp...  4.4 us
    all_to_all x1, starting transfers between devices, on_device(): lax.all_to_all(homeward, 'expert', split_axis=0, concat_axis=0, tiled=True)  3.77 us
    scatter-add x1, other arithmetic, on_device(): combined = jax.ops.segment_sum(scaled, slot_token, num_segments=tok_rows)  3.58 us
  transfers between devices with their start and end apart: 2, of which 2 were waited for; matrix products, arithmetic and copies ran while one was open for 2% of the time, Pallas kernels for 0%

commit v1 on v0

v1 whole, which is shorter than its diff:
```python
import jax
import jax.numpy as jnp
from jax import lax
from jax.experimental import pallas as pl
from jax.experimental.pallas import tpu as pltpu
from jax.sharding import PartitionSpec as P

BF16, F32 = jnp.bfloat16, jnp.float32


def slot_onehot(ids, flight, capacity):
    top, tok = ids.shape
    experts = lax.broadcasted_iota(jnp.int32, (flight, tok), 0)
    chosen = jnp.zeros((flight, tok), F32)
    for k in range(top):
        chosen = jnp.where(ids[k : k + 1, :] == experts, 1.0, chosen)
    before = lax.broadcasted_iota(jnp.int32, (tok, tok), 0) < lax.broadcasted_iota(
        jnp.int32, (tok, tok), 1
    )
    rank = jnp.dot(
        chosen.astype(BF16), before.astype(F32).astype(BF16), preferred_element_type=F32
    )
    rank = jnp.where(chosen > 0.5, rank, -1.0)
    places = lax.broadcasted_iota(jnp.int32, (flight, capacity, tok), 1).astype(F32)
    return rank[:, None, :] == places


def dispatch_kernel(flight, capacity, ids_ref, tokens_ref, out_ref):
    tok = ids_ref.shape[1]
    picked = slot_onehot(ids_ref[...], flight, capacity)
    onehot = jnp.where(picked, 1.0, 0.0).reshape(flight * capacity, tok).astype(BF16)
    out_ref[...] = jnp.dot(onehot, tokens_ref[...], preferred_element_type=F32).astype(BF16)


def combine_kernel(flight, capacity, ids_ref, weights_ref, rows_ref, out_ref):
    ids = ids_ref[...]
    top, tok = ids.shape
    picked = slot_onehot(ids, flight, capacity)
    experts = lax.broadcasted_iota(jnp.int32, (flight, tok), 0)
    weight = jnp.zeros((flight, tok), F32)
    for k in range(top):
        weight = jnp.where(ids[k : k + 1, :] == experts, weights_ref[k : k + 1, :], weight)
    mix = jnp.where(picked, weight[:, None, :], 0.0).reshape(flight * capacity, tok)
    total = None
    for _ in range(3):
        part = mix.astype(BF16)
        mix = mix - part.astype(F32)
        term = lax.dot_general(
            part, rows_ref[...], (((0,), (0,)), ((), ())), preferred_element_type=F32
        )
        total = term if total is None else total + term
    out_ref[...] = total.astype(BF16)


def matmul_kernel(finish, half_ref, x_ref, w_ref, *refs):
    out_ref, acc = refs[-2], refs[-1]
    step = pl.program_id(0)
    term = jnp.dot(x_ref[...], w_ref[0], preferred_element_type=F32)

    @pl.when(step == 0)
    def _():
        acc[...] = term if len(refs) == 2 else refs[0][...] + term

    @pl.when(step > 0)
    def _():
        acc[...] += term

    @pl.when(step == pl.num_programs(0) - 1)
    def _():
        out_ref[...] = finish(acc[...]).astype(out_ref.dtype)


def matmul_rows(half, x, w, start, finish, dtype, block):
    rows, depth = x.shape
    width = w.shape[2]
    steps = depth // block
    whole = pl.BlockSpec((rows, width), lambda k, h: (0, 0))
    return pl.pallas_call(
        lambda *refs: matmul_kernel(finish, *refs),
        grid_spec=pltpu.PrefetchScalarGridSpec(
            num_scalar_prefetch=1,
            grid=(steps,),
            in_specs=[
                pl.BlockSpec((rows, block), lambda k, h: (0, k)),
                pl.BlockSpec((1, block, width), lambda k, h: (0, h[0] * steps + k, 0)),
            ]
            + ([] if start is None else [whole]),
            out_specs=whole,
            scratch_shapes=[pltpu.VMEM((rows, width), F32)],
        ),
        out_shape=jax.ShapeDtypeStruct((rows, width), dtype),
        compiler_params=pltpu.CompilerParams(vmem_limit_bytes=48 * 2**20),
    )(half, x, w, *([] if start is None else [start]))


def silu(v):
    return v / (1.0 + jnp.exp(-v))


def same(v):
    return v


def on_device(tokens, expert_ids, route_weights, up_proj, down_proj):
    tok_rows, width = tokens.shape
    capacity = tok_rows // 16
    owners = lax.axis_size("expert")
    loops = lax.axis_size("loop")
    per_owner = up_proj.shape[0]
    flight = owners * per_owner
    slots = flight * capacity
    ids_t, weights_t = expert_ids.T, route_weights.T

    outgoing = pl.pallas_call(
        lambda *refs: dispatch_kernel(flight, capacity, *refs),
        out_shape=jax.ShapeDtypeStruct((slots, width), BF16),
    )(ids_t, tokens)
    arrived = lax.all_to_all(
        outgoing.reshape(owners, per_owner * capacity, width),
        "expert",
        split_axis=0,
        concat_axis=0,
        tiled=True,
    ).reshape(slots, width)

    me = lax.axis_index("loop").astype(jnp.int32).reshape(1)
    if loops == 2:
        swap = [(0, 1), (1, 0)]
        other = lax.ppermute(arrived, "loop", swap)
        up_block = width // 7
        part = matmul_rows(me, arrived, up_proj, None, same, F32, up_block)
        hidden = matmul_rows(1 - me, other, up_proj, part, silu, BF16, up_block)
        hidden_other = lax.ppermute(hidden, "loop", swap)
        part = matmul_rows(me, hidden, down_proj, None, same, F32, hidden.shape[1] // 4)
        out_rows = matmul_rows(
            1 - me, hidden_other, down_proj, part, same, BF16, hidden.shape[1] // 4
        )
    else:
        full = lax.all_gather(arrived, "loop", axis=1, tiled=True)
        zero = jnp.zeros_like(me)
        hidden = matmul_rows(zero, full, up_proj, None, silu, BF16, full.shape[1] // 7)
        hidden_full = lax.all_gather(hidden, "loop", axis=1, tiled=True)
        out_rows = matmul_rows(zero, hidden_full, down_proj, None, same, BF16, hidden_full.shape[1] // 8)

    returned = lax.all_to_all(
        out_rows.reshape(owners, per_owner * capacity, width),
        "expert",
        split_axis=0,
        concat_axis=0,
        tiled=True,
    ).reshape(slots, width)
    return pl.pallas_call(
        lambda *refs: combine_kernel(flight, capacity, *refs),
        out_shape=jax.ShapeDtypeStruct((tok_rows, width), BF16),
    )(ids_t, weights_t, returned)


def solution(mesh):
    return jax.shard_map(
        on_device,
        mesh=mesh,
        in_specs=(
            P("expert", "loop"),
            P("expert", None),
            P("expert", None),
            P("expert", None, "loop"),
            P("expert", None, "loop"),
        ),
        out_specs=P("expert", "loop"),
        check_vma=False,
    )
```

time: 125 us -> 86.1 us (0.69)
  waiting for transfers between devices: 35.3 us -> 0.01 us
  Pallas kernels: 0 us -> 25.1 us
  between operations: 13.5 us -> 0.05 us
  blocking collectives: 53.1 us -> 59.7 us
  other arithmetic: 6.58 us -> 0 us
  matrix products: 6.47 us -> 0 us
  local copies, waits for them, and re-layouts: 5.53 us -> 0 us
  starting transfers between devices: 3.77 us -> 0.57 us
    pallas_call x0 -> x6, Pallas kernels: none -> 25.1 us  [the longest x4 19.3 us: matmul_rows(): pl.pallas_call(lambda *refs: matmul_kernel(finish, *refs), grid_spec=pltp...]
    all_to_all x1 -> x0, waiting for transfers between devices: 22 us -> none  [on_device(): lax.all_to_all(homeward, 'expert', split_axis=0, concat_axis=0, tiled=True)]
    all_gather x1 -> x0, waiting for transfers between devices: 12.6 us -> none  [on_device(): features = lax.all_gather(tokens, 'loop', axis=1, tiled=True)]
    all_to_all x1 -> x2, blocking collectives: 51.1 us -> 59.7 us  [the longest x1 32.1 us: on_device(): lax.all_to_all(outgoing.reshape(owners, per_owner * capacity, width), 'ex...]
    dot_general x2 -> x0, matrix products: 6.47 us -> none  [the longest x1 4.4 us: on_device(): jnp.einsum('esd,edh->esh', slot_rows, up_proj, preferred_element_type=jnp...]
    gather x1 -> x0, local copies, waits for them, and re-layouts: 5.1 us -> none  [on_device(): jnp.take(features, slot_token, axis=0) * live_mask]
    all_to_all x1 -> x0, starting transfers between devices: 3.77 us -> none  [on_device(): lax.all_to_all(homeward, 'expert', split_axis=0, concat_axis=0, tiled=True)]
    scatter-add x1 -> x0, other arithmetic: 3.58 us -> none  [on_device(): combined = jax.ops.segment_sum(scaled, slot_token, num_segments=tok_rows)]
  transfers between devices with their start and end apart: 2 -> 2, of which waited for: 2 -> 0; matrix products, arithmetic and copies ran while one was open for 2% -> 0% of each run, Pallas kernels for 0% -> 11%
where the time goes in v1:
time: 86.1 us; the launch traced here: 85.5 us
  blocking collectives  59.7 us (69%)
  Pallas kernels  25.1 us (29%)
    all_to_all x1, blocking collectives, on_device(): lax.all_to_all(outgoing.reshape(owners, per_owner * capacity, width), 'ex...  32.1 us
    all_to_all x1, blocking collectives, on_device(): lax.all_to_all(out_rows.reshape(owners, per_owner * capacity, width), 'ex...  27.6 us
    pallas_call x4, Pallas kernels, matmul_rows(): pl.pallas_call(lambda *refs: matmul_kernel(finish, *refs), grid_spec=pltp...  19.3 us
    pallas_call x1, Pallas kernels, on_device(): pl.pallas_call(lambda *refs: combine_kernel(flight, capacity, *refs), out...  3.19 us
    pallas_call x1, Pallas kernels, on_device(): pl.pallas_call(lambda *refs: dispatch_kernel(flight, capacity, *refs), ou...  2.63 us
  transfers between devices with their start and end apart: 2, of which 0 were waited for; matrix products, arithmetic and copies ran while one was open for 0% of the time, Pallas kernels for 11%

profile of v1, /device:TPU:0, one launch (start us, length us, event | category | flops | bytes accessed | tf_op | source)
XLA Modules:
  0.0 85.5 jit_solution(8840762319811020644)
XLA Ops:
  0.0 2.6 %shard_map.55 = bf16[128,3584]{1,0:T(8,128)(2,1)} custom-call(s32[8,128]{1,0:T(8,128)} %bitcast.12, bf16[128,3584]{1,0:T(8,128)(2,1)} %refs_1_.1), custom_call_target="tpu_custom_call" | custom-call | tf_op jit(solution)/shard_map/pallas_call | solution.py:114
  2.6 32.1 %all_to_all.10 = bf16[16,8,3584]{2,1,0:T(8,128)(2,1)S(1)} all-to-all(bf16[16,8,3584]{2,1,0:T(8,128)(2,1)} %bitcast.11), channel_id=1, replica_groups=mesh['expert'=16,'loop'=2] {'expert'}, dimensions={0} | all-to-all | bytes 1835008 | tf_op jit(solution)/shard_map/all_to_all | solution.py:118
  34.8 0.0 collective-permute-start
  34.8 5.3 %shard_map.56.refs_3_ = f32[128,512]{1,0:T(8,128)S(1)} custom-call(s32[1]{0:T(128)} %bitcast.2.refs_0_, bf16[128,3584]{1,0:T(8,128)(2,1)S(1)} %bitcast.8, bf16[1,7168,512]{2,1,0:T(8,128)(2,1)} %refs_2_.5), custom_call_target="tpu_custom_call" | custom-call | tf_op jit(solution)/shard_map/pallas_call | solution.py:78
  40.1 0.0 collective-permute-done.refs_1_
  40.1 5.4 %shard_map.57.refs_1_ = bf16[128,512]{1,0:T(8,128)(2,1)S(1)} custom-call(s32[1]{0:T(128)S(6)} %sub.4.refs_0_, bf16[128,3584]{1,0:T(8,128)(2,1)S(1)} %collective-permute-done.refs_1_, bf16[1,7168,512]{2,1,0:T(8,128)(2,1)} %refs_2_.5, f32[128,512]{1,0:T(8,128)S(1)} %shard_map.56.refs_3_), custom_call_target="tpu_custom_call" | custom-call | tf_op jit(solution)/shard_map/pallas_call | solution.py:78
  45.6 0.6 collective-permute-start.1
  46.1 4.2 %shard_map.58.refs_3_ = f32[128,3584]{1,0:T(8,128)S(1)} custom-call(s32[1]{0:T(128)} %bitcast.2.refs_0_, bf16[128,512]{1,0:T(8,128)(2,1)S(1)} %shard_map.57.refs_1_, bf16[1,1024,3584]{2,1,0:T(8,128)(2,1)} %refs_2_.7), custom_call_target="tpu_custom_call" | custom-call | tf_op jit(solution)/shard_map/pallas_call | solution.py:78
  50.4 0.0 collective-permute-done.1.refs_1_
  50.4 4.3 %shard_map.59 = bf16[128,3584]{1,0:T(8,128)(2,1)S(1)} custom-call(s32[1]{0:T(128)S(6)} %sub.4.refs_0_, bf16[128,512]{1,0:T(8,128)(2,1)S(1)} %collective-permute-done.1.refs_1_, bf16[1,1024,3584]{2,1,0:T(8,128)(2,1)} %refs_2_.7, f32[128,3584]{1,0:T(8,128)S(1)} %shard_map.58.refs_3_), custom_call_target="tpu_custom_call" | custom-call | tf_op jit(solution)/shard_map/pallas_call | solution.py:78
  54.7 27.6 %all_to_all.11 = bf16[16,8,3584]{2,1,0:T(8,128)(2,1)} all-to-all(bf16[16,8,3584]{2,1,0:T(8,128)(2,1)S(1)} %bitcast.9), channel_id=1, replica_groups=mesh['expert'=16,'loop'=2] {'expert'}, dimensions={0} | all-to-all | bytes 1835008 | tf_op jit(solution)/shard_map/all_to_all | solution.py:145
  82.3 3.2 %shard_map.60 = bf16[128,3584]{1,0:T(8,128)(2,1)} custom-call(s32[8,128]{1,0:T(8,128)} %bitcast.13, f32[8,128]{1,0:T(8,128)} %bitcast.14, bf16[128,3584]{1,0:T(8,128)(2,1)} %bitcast.10), custom_call_target="tpu_custom_call" | custom-call | tf_op jit(solution)/shard_map/pallas_call | solution.py:152
Async XLA Ops:
  34.8 5.3 %collective-permute-start = (bf16[128,3584]{1,0:T(8,128)(2,1)S(1)}, bf16[128,3584]{1,0:T(8,128)(2,1)S(1)}, u32[]{:S(2)}, u32[]{:S(2)}) collective-permute-start(bf16[128,3584]{1,0:T(8,128)(2,1)S(1)} %bitcast.7), channel_id=1, source_target_pairs={{0,1},{1,0},{2,3},{3,2},{4,5},{5,4},{6,7},{7,6},{8,9},{9,8},{10,11... | collective-permute-start | bytes 2752520 | tf_op jit(solution)/shard_map/ppermute | solution.py:129
  45.6 4.8 %collective-permute-start.1 = (bf16[128,512]{1,0:T(8,128)(2,1)S(1)}, bf16[128,512]{1,0:T(8,128)(2,1)S(1)}, u32[]{:S(2)}, u32[]{:S(2)}) collective-permute-start(bf16[128,512]{1,0:T(8,128)(2,1)S(1)} %shard_map.57.refs_1_), channel_id=1, source_target_pairs={{0,1},{1,0},{2,3},{3,2},{4,5},{5,4},{6,7},{7,6},{8,9},{9,8},{10,11... | collective-permute-start | bytes 393224 | tf_op jit(solution)/shard_map/ppermute | solution.py:133

commit v2 on v1

--- a/solution.py
+++ b/solution.py
@@ -52,53 +52,44 @@
     out_ref[...] = total.astype(BF16)
 
 
-def matmul_kernel(finish, half_ref, x_ref, w_ref, *refs):
-    out_ref, acc = refs[-2], refs[-1]
-    step = pl.program_id(0)
-    term = jnp.dot(x_ref[...], w_ref[0], preferred_element_type=F32)
-
-    @pl.when(step == 0)
-    def _():
-        acc[...] = term if len(refs) == 2 else refs[0][...] + term
-
-    @pl.when(step > 0)
-    def _():
-        acc[...] += term
-
-    @pl.when(step == pl.num_programs(0) - 1)
-    def _():
-        out_ref[...] = finish(acc[...]).astype(out_ref.dtype)
+def whole_call(kernel, shape, dtype, *arrays):
+    return pl.pallas_call(
+        kernel,
+        in_specs=[pl.BlockSpec(memory_space=pltpu.VMEM)] * len(arrays),
+        out_specs=pl.BlockSpec(memory_space=pltpu.VMEM),
+        out_shape=jax.ShapeDtypeStruct(shape, dtype),
+        compiler_params=pltpu.CompilerParams(vmem_limit_bytes=16 * 2**20),
+    )(*arrays)
 
 
-def matmul_rows(half, x, w, start, finish, dtype, block):
-    rows, depth = x.shape
-    width = w.shape[2]
-    steps = depth // block
-    whole = pl.BlockSpec((rows, width), lambda k, h: (0, 0))
-    return pl.pallas_call(
-        lambda *refs: matmul_kernel(finish, *refs),
-        grid_spec=pltpu.PrefetchScalarGridSpec(
-            num_scalar_prefetch=1,
-            grid=(steps,),
-            in_specs=[
-                pl.BlockSpec((rows, block), lambda k, h: (0, k)),
-                pl.BlockSpec((1, block, width), lambda k, h: (0, h[0] * steps + k, 0)),
-            ]
-            + ([] if start is None else [whole]),
-            out_specs=whole,
-            scratch_shapes=[pltpu.VMEM((rows, width), F32)],
-        ),
-        out_shape=jax.ShapeDtypeStruct((rows, width), dtype),
-        compiler_params=pltpu.CompilerParams(vmem_limit_bytes=48 * 2**20),
-    )(half, x, w, *([] if start is None else [start]))
+def half_dot(x_ref, w_ref, core):
+    depth = x_ref.shape[1]
+    rows = pl.ds(pl.multiple_of(core * depth, depth), depth)
+    return jnp.dot(x_ref[...], w_ref[0, rows, :], preferred_element_type=F32)
+
+
+def mine_kernel(x_ref, w_ref, out_ref):
+    out_ref[...] = half_dot(x_ref, w_ref, lax.axis_index("loop"))
+
+
+def up_kernel(part_ref, x_ref, w_ref, out_ref):
+    out_ref[...] = silu(part_ref[...] + half_dot(x_ref, w_ref, 1 - lax.axis_index("loop"))).astype(BF16)
+
+
+def down_kernel(part_ref, x_ref, w_ref, out_ref):
+    out_ref[...] = (part_ref[...] + half_dot(x_ref, w_ref, 1 - lax.axis_index("loop"))).astype(BF16)
+
+
+def plain_up_kernel(x_ref, w_ref, out_ref):
+    out_ref[...] = silu(jnp.dot(x_ref[...], w_ref[0], preferred_element_type=F32)).astype(BF16)
+
+
+def plain_down_kernel(x_ref, w_ref, out_ref):
+    out_ref[...] = jnp.dot(x_ref[...], w_ref[0], preferred_element_type=F32).astype(BF16)
 
 
 def silu(v):
     return v / (1.0 + jnp.exp(-v))
-
-
-def same(v):
-    return v
 
 
 def on_device(tokens, expert_ids, route_weights, up_proj, down_proj):
@@ -114,6 +105,8 @@
     outgoing = pl.pallas_call(
         lambda *refs: dispatch_kernel(flight, capacity, *refs),
         out_shape=jax.ShapeDtypeStruct((slots, width), BF16),
+        cost_estimate=pl.CostEstimate(flops=10**11, bytes_accessed=10**8, transcendentals=0),
+        compiler_params=pltpu.CompilerParams(vmem_limit_bytes=16 * 2**20),
     )(ids_t, tokens)
     arrived = lax.all_to_all(
         outgoing.reshape(owners, per_owner * capacity, width),
@@ -123,24 +116,20 @@
         tiled=True,
     ).reshape(slots, width)
 
-    me = lax.axis_index("loop").astype(jnp.int32).reshape(1)
     if loops == 2:
         swap = [(0, 1), (1, 0)]
-        other = lax.ppermute(arrived, "loop", swap)
-        up_block = width // 7
-        part = matmul_rows(me, arrived, up_proj, None, same, F32, up_block)
-        hidden = matmul_rows(1 - me, other, up_proj, part, silu, BF16, up_block)
-        hidden_other = lax.ppermute(hidden, "loop", swap)
-        part = matmul_rows(me, hidden, down_proj, None, same, F32, hidden.shape[1] // 4)
-        out_rows = matmul_rows(
-            1 - me, hidden_other, down_proj, part, same, BF16, hidden.shape[1] // 4
-        )
+        theirs = lax.ppermute(arrived, "loop", swap)
+        units = up_proj.shape[2]
+        part = whole_call(mine_kernel, (slots, units), F32, arrived, up_proj)
+        hidden = whole_call(up_kernel, (slots, units), BF16, part, theirs, up_proj)
+        hidden_theirs = lax.ppermute(hidden, "loop", swap)
+        part = whole_call(mine_kernel, (slots, width), F32, hidden, down_proj)
+        out_rows = whole_call(down_kernel, (slots, width), BF16, part, hidden_theirs, down_proj)
     else:
         full = lax.all_gather(arrived, "loop", axis=1, tiled=True)
-        zero = jnp.zeros_like(me)
-        hidden = matmul_rows(zero, full, up_proj, None, silu, BF16, full.shape[1] // 7)
-        hidden_full = lax.all_gather(hidden, "loop", axis=1, tiled=True)
-        out_rows = matmul_rows(zero, hidden_full, down_proj, None, same, BF16, hidden_full.shape[1] // 8)
+        hidden = whole_call(plain_up_kernel, (slots, up_proj.shape[2]), BF16, full, up_proj)
+        hidden = lax.all_gather(hidden, "loop", axis=1, tiled=True)
+        out_rows = whole_call(plain_down_kernel, (slots, width), BF16, hidden, down_proj)
 
     returned = lax.all_to_all(
         out_rows.reshape(owners, per_owner * capacity, width),
@@ -152,6 +141,7 @@
     return pl.pallas_call(
         lambda *refs: combine_kernel(flight, capacity, *refs),
         out_shape=jax.ShapeDtypeStruct((tok_rows, width), BF16),
+        compiler_params=pltpu.CompilerParams(vmem_limit_bytes=16 * 2**20),
     )(ids_t, weights_t, returned)
 
 

time: 86.1 us -> 69.6 us (0.81)
  Pallas kernels: 25.1 us -> 5.11 us
  waiting for transfers between devices: 0.01 us -> 2.33 us
  local copies, waits for them, and re-layouts: 0 us -> 1.89 us
    pallas_call x4, Pallas kernels: 19.3 us -> 2.62 us  [whole_call(): pl.pallas_call(kernel, in_specs=[pl.BlockSpec(memory_space=pltpu.VMEM)] *...]
    ppermute x2, waiting for transfers between devices: 0.01 us -> 2.33 us  [the longest x1 1.8 us: on_device(): theirs = lax.ppermute(arrived, 'loop', swap)]
    pallas_call x1, Pallas kernels: 2.63 us -> 0.51 us  [on_device(): pl.pallas_call(lambda *refs: dispatch_kernel(flight, capacity, *refs), ou...]
    unnamed x0 -> x14, local copies, waits for them, and re-layouts: none -> 1.89 us
    pallas_call x1, Pallas kernels: 3.19 us -> 1.97 us  [on_device(): pl.pallas_call(lambda *refs: combine_kernel(flight, capacity, *refs), out...]
  transfers between devices with their start and end apart: 2 -> 2, of which waited for: 0 -> 2; matrix products, arithmetic and copies ran while one was open for 0% -> 0% of each run, Pallas kernels for 11% -> 2%
where the time goes in v2:
time: 69.6 us; the launch traced here: 69.4 us
  blocking collectives  59.8 us (86%)
  Pallas kernels  5.11 us (7%)
  waiting for transfers between devices  2.33 us (3%)
  local copies, waits for them, and re-layouts  1.89 us (3%)
    all_to_all x1, blocking collectives, on_device(): lax.all_to_all(outgoing.reshape(owners, per_owner * capacity, width), 'ex...  32.2 us
    all_to_all x1, blocking collectives, on_device(): lax.all_to_all(out_rows.reshape(owners, per_owner * capacity, width), 'ex...  27.6 us
    pallas_call x4, Pallas kernels, whole_call(): pl.pallas_call(kernel, in_specs=[pl.BlockSpec(memory_space=pltpu.VMEM)] *...  2.62 us
    pallas_call x1, Pallas kernels, on_device(): pl.pallas_call(lambda *refs: combine_kernel(flight, capacity, *refs), out...  1.97 us
    unnamed x14, local copies, waits for them, and re-layouts  1.89 us
    ppermute x1, waiting for transfers between devices, on_device(): theirs = lax.ppermute(arrived, 'loop', swap)  1.8 us
  transfers between devices with their start and end apart: 2, of which 2 were waited for; matrix products, arithmetic and copies ran while one was open for 0% of the time, Pallas kernels for 2%

profile of v2, /device:TPU:0, one launch (start us, length us, event | category | flops | bytes accessed | tf_op | source)
XLA Modules:
  0.0 69.4 jit_solution(5079324063134350039)
XLA Ops:
  0.0 0.0 copy-start.1
  0.0 0.7 copy-done.1
  0.7 0.0 copy-start.4
  0.7 1.2 %copy-done.4 = bf16[128,3584]{1,0:T(8,128)(2,1)S(1)} copy-done((bf16[128,3584]{1,0:T(8,128)(2,1)S(1)}, bf16[128,3584]{1,0:T(8,128)(2,1)}, u32[]{:S(2)}) %copy-start.4) | copy-done | bytes 917528
  1.9 0.0 copy-start
  1.9 0.5 shard_map.55
  2.4 32.2 %all_to_all.10 = bf16[16,8,3584]{2,1,0:T(8,128)(2,1)S(1)} all-to-all(bf16[16,8,3584]{2,1,0:T(8,128)(2,1)S(1)} %bitcast.12), channel_id=1, replica_groups=mesh['expert'=16,'loop'=2] {'expert'}, dimensions={0} | all-to-all | bytes 1835008 | tf_op jit(solution)/shard_map/all_to_all | solution.py:111
  34.6 0.0 slice-start
  34.6 0.0 collective-permute-start
  34.6 0.0 copy-done
  34.6 0.6 shard_map.56.part_ref
  35.3 0.0 slice-start.1
  35.3 1.8 %collective-permute-done.x_ref = bf16[128,3584]{1,0:T(8,128)(2,1)S(1)} collective-permute-done((bf16[128,3584]{1,0:T(8,128)(2,1)S(1)}, bf16[128,3584]{1,0:T(8,128)(2,1)S(1)}, u32[]{:S(2)}, u32[]{:S(2)}) %collective-permute-start) | collective-permute-done | bytes 917536 | tf_op jit(solution)/shard_map/ppermute | solution.py:121
  37.1 0.7 shard_map.57.x_ref
  37.8 0.2 collective-permute-start.1
  38.0 0.0 slice-done
  38.0 0.0 slice-done.1
  38.0 0.6 shard_map.58.part_ref
  38.6 0.0 copy-start.2
  38.6 0.0 copy-start.3
  38.6 0.5 collective-permute-done.1.x_ref
  39.2 0.6 shard_map.59
  39.8 27.6 %all_to_all.11 = bf16[16,8,3584]{2,1,0:T(8,128)(2,1)S(1)} all-to-all(bf16[16,8,3584]{2,1,0:T(8,128)(2,1)S(1)} %bitcast.10), channel_id=1, replica_groups=mesh['expert'=16,'loop'=2] {'expert'}, dimensions={0} | all-to-all | bytes 1835008 | tf_op jit(solution)/shard_map/all_to_all | solution.py:134
  67.4 0.0 copy-done.2
  67.4 0.0 copy-done.3
  67.4 2.0 %shard_map.60 = bf16[128,3584]{1,0:T(8,128)(2,1)} custom-call(s32[8,128]{1,0:T(8,128)S(1)} %bitcast.14, f32[8,128]{1,0:T(8,128)S(1)} %bitcast.15, bf16[128,3584]{1,0:T(8,128)(2,1)S(1)} %bitcast.11), custom_call_target="tpu_custom_call" | custom-call | tf_op jit(solution)/shard_map/pallas_call | solution.py:141
  (1 shorter events, 0.0 us)
Async XLA Ops:
  0.0 0.7 copy-start.1
  0.7 1.2 %copy-start.4 = (bf16[128,3584]{1,0:T(8,128)(2,1)S(1)}, bf16[128,3584]{1,0:T(8,128)(2,1)}, u32[]{:S(2)}) copy-start(bf16[128,3584]{1,0:T(8,128)(2,1)} %refs_1_.1) | copy-start | bytes 2752516
  1.9 32.7 %copy-start = (bf16[1,7168,512]{2,1,0:T(8,128)(2,1)S(1)}, bf16[1,7168,512]{2,1,0:T(8,128)(2,1)}, u32[]{:S(2)}) copy-start(bf16[1,7168,512]{2,1,0:T(8,128)(2,1)} %w_ref.5) | copy-start | bytes 22020100
  34.6 3.4 %slice-start = ((s8[7340032]{0:T(1024)(128)(4,1)}), s8[4194304]{0:T(1024)(128)(4,1)S(1)}, s32[]{:S(2)}) async-start(s8[7340032]{0:T(1024)(128)(4,1)} %bitcast.6), calls=%async_computation.2 | async-start | bytes 8388608
  34.6 2.5 %collective-permute-start = (bf16[128,3584]{1,0:T(8,128)(2,1)S(1)}, bf16[128,3584]{1,0:T(8,128)(2,1)S(1)}, u32[]{:S(2)}, u32[]{:S(2)}) collective-permute-start(bf16[128,3584]{1,0:T(8,128)(2,1)S(1)} %bitcast.8), channel_id=1, source_target_pairs={{0,1},{1,0},{2,3},{3,2},{4,5},{5,4},{6,7},{7,6},{8,9},{9,8},{10,11... | collective-permute-start | bytes 2752520 | tf_op jit(solution)/shard_map/ppermute | solution.py:121
  35.3 2.7 %slice-start.1 = ((s8[7340032]{0:T(1024)(128)(4,1)}), s8[3145728]{0:T(1024)(128)(4,1)S(1)}, s32[]{:S(2)}) async-start(s8[7340032]{0:T(1024)(128)(4,1)} %bitcast.6), calls=%async_computation.3 | async-start | bytes 6291456
  37.8 1.4 %collective-permute-start.1 = (bf16[128,512]{1,0:T(8,128)(2,1)S(1)}, bf16[128,512]{1,0:T(8,128)(2,1)S(1)}, u32[]{:S(2)}, u32[]{:S(2)}) collective-permute-start(bf16[128,512]{1,0:T(8,128)(2,1)S(1)} %shard_map.57.x_ref), channel_id=1, source_target_pairs={{0,1},{1,0},{2,3},{3,2},{4,5},{5,4},{6,7},{7,6},{8,9},{9,8},{10,11... | collective-permute-start | bytes 393224 | tf_op jit(solution)/shard_map/ppermute | solution.py:125
  38.6 28.8 %copy-start.2 = (s32[128,8]{0,1:T(8,128)S(1)}, s32[128,8]{0,1:T(8,128)}, u32[]{:S(2)}) copy-start(s32[128,8]{0,1:T(8,128)} %param.6) | copy-start | bytes 12292
  38.6 28.8 %copy-start.3 = (f32[128,8]{0,1:T(8,128)S(1)}, f32[128,8]{0,1:T(8,128)}, u32[]{:S(2)}) copy-start(f32[128,8]{0,1:T(8,128)} %param.7) | copy-start | bytes 12292

commit v3 on v2

v3 whole, which is shorter than its diff:
```python
import jax
import jax.numpy as jnp
from jax import lax
from jax.experimental import pallas as pl
from jax.experimental.pallas import tpu as pltpu
from jax.sharding import PartitionSpec as P

BF16, F32 = jnp.bfloat16, jnp.float32
COMBINE_BLOCKS, MIX_PARTS = 7, 2


def slot_tables(ids_ref, weights_ref, onehot_ref, mix_ref, flight, capacity):
    top, tok = ids_ref.shape
    experts = lax.broadcasted_iota(jnp.int32, (flight, tok), 0)
    chosen = jnp.zeros((flight, tok), F32)
    weight = jnp.zeros((flight, tok), F32)
    for k in range(top):
        names = ids_ref[k : k + 1, :] == experts
        chosen = jnp.where(names, 1.0, chosen)
        weight = jnp.where(names, weights_ref[k : k + 1, :], weight)
    before = lax.broadcasted_iota(jnp.int32, (tok, tok), 0) < lax.broadcasted_iota(
        jnp.int32, (tok, tok), 1
    )
    rank = jnp.dot(
        chosen.astype(BF16), jnp.where(before, 1.0, 0.0).astype(BF16), preferred_element_type=F32
    )
    rank = jnp.where(chosen > 0.5, rank, -1.0)
    places = lax.broadcasted_iota(jnp.int32, (flight, capacity, tok), 1).astype(F32)
    picked = rank[:, None, :] == places
    onehot_ref[...] = jnp.where(picked, 1.0, 0.0).reshape(flight * capacity, tok).astype(BF16)
    mix = jnp.where(picked, weight[:, None, :], 0.0).reshape(flight * capacity, tok).T
    for i in range(MIX_PARTS):
        part = mix.astype(BF16)
        mix_ref[i] = part
        mix = mix - part.astype(F32)


def column_blocks(width, count):
    block = width // count
    return [slice(i * block, (i + 1) * block) for i in range(count)]


def read_kernel(
    flight, capacity, ids_ref, weights_ref, tokens_ref, held, onehot_ref, mix_ref, ids, weights, sems
):
    copies = [
        pltpu.make_async_copy(ids_ref, ids, sems.at[0]),
        pltpu.make_async_copy(weights_ref, weights, sems.at[1]),
        pltpu.make_async_copy(tokens_ref, held, sems.at[2]),
    ]
    for copy in copies:
        copy.start()
    copies[0].wait()
    copies[1].wait()
    slot_tables(ids, weights, onehot_ref, mix_ref, flight, capacity)
    copies[2].wait()


def pick_kernel(onehot_ref, held_ref, out_ref):
    out_ref[...] = jnp.dot(onehot_ref[...], held_ref[...], preferred_element_type=F32).astype(BF16)


def dispatch(ids_t, weights_t, tokens, flight, capacity):
    hbm = pl.BlockSpec(memory_space=pltpu.HBM)
    vmem = pl.BlockSpec(memory_space=pltpu.VMEM)
    slots, tok = flight * capacity, tokens.shape[0]
    held, onehot, mix = pl.pallas_call(
        lambda *refs: read_kernel(flight, capacity, *refs),
        in_specs=[hbm, hbm, hbm],
        out_specs=[vmem, vmem, vmem],
        out_shape=[
            jax.ShapeDtypeStruct(tokens.shape, BF16),
            jax.ShapeDtypeStruct((slots, tok), BF16),
            jax.ShapeDtypeStruct((MIX_PARTS, tok, slots), BF16),
        ],
        scratch_shapes=[
            pltpu.VMEM(ids_t.shape, jnp.int32),
            pltpu.VMEM(weights_t.shape, F32),
            pltpu.SemaphoreType.DMA((3,)),
        ],
        cost_estimate=pl.CostEstimate(flops=0, bytes_accessed=0, transcendentals=0),
        compiler_params=pltpu.CompilerParams(vmem_limit_bytes=16 * 2**20),
    )(*(pltpu.with_memory_space_constraint(a, pltpu.HBM) for a in (ids_t, weights_t, tokens)))
    outgoing = pl.pallas_call(
        pick_kernel,
        in_specs=[vmem, vmem],
        out_specs=vmem,
        out_shape=jax.ShapeDtypeStruct((slots, tokens.shape[1]), BF16),
        cost_estimate=pl.CostEstimate(flops=10**11, bytes_accessed=10**8, transcendentals=0),
        compiler_params=pltpu.CompilerParams(vmem_limit_bytes=16 * 2**20),
    )(onehot, held)
    return outgoing, mix


def combine_kernel(mix_ref, rows_ref, out_ref, held, sems):
    copies = []
    for i, at in enumerate(column_blocks(held.shape[1], COMBINE_BLOCKS)):
        rows = rows_ref[:, at]
        held[:, at] = sum(
            jnp.dot(mix_ref[k], rows, preferred_element_type=F32) for k in range(MIX_PARTS)
        ).astype(BF16)
        copies.append(pltpu.make_async_copy(held.at[:, at], out_ref.at[:, at], sems.at[i]))
        copies[-1].start()
    for copy in copies:
        copy.wait()


def combine(mix, rows):
    tok, width = mix.shape[1], rows.shape[1]
    vmem = pl.BlockSpec(memory_space=pltpu.VMEM)
    return pl.pallas_call(
        combine_kernel,
        in_specs=[vmem, vmem],
        out_specs=pl.BlockSpec(memory_space=pltpu.HBM),
        out_shape=jax.ShapeDtypeStruct((tok, width), BF16),
        scratch_shapes=[
            pltpu.VMEM((tok, width), BF16),
            pltpu.SemaphoreType.DMA((COMBINE_BLOCKS,)),
        ],
        compiler_params=pltpu.CompilerParams(vmem_limit_bytes=16 * 2**20),
    )(mix, rows)


def whole_call(kernel, out, *arrays):
    return pl.pallas_call(
        kernel,
        in_specs=[pl.BlockSpec(memory_space=pltpu.VMEM)] * len(arrays),
        out_specs=jax.tree.map(lambda _: pl.BlockSpec(memory_space=pltpu.VMEM), out),
        out_shape=out,
        cost_estimate=pl.CostEstimate(flops=2**29, bytes_accessed=0, transcendentals=0),
        compiler_params=pltpu.CompilerParams(vmem_limit_bytes=16 * 2**20),
    )(*arrays)


def half_dot(x_ref, w_ref, core):
    depth = x_ref.shape[1]
    rows = pl.ds(pl.multiple_of(core * depth, depth), depth)
    return jnp.dot(x_ref[...], w_ref[0, rows, :], preferred_element_type=F32)


def mine_kernel(x_ref, w_ref, out_ref):
    out_ref[...] = half_dot(x_ref, w_ref, lax.axis_index("loop"))


def up_kernel(part_ref, x_ref, w_ref, out_ref):
    out_ref[...] = silu(part_ref[...] + half_dot(x_ref, w_ref, 1 - lax.axis_index("loop"))).astype(BF16)


def down_kernel(part_ref, x_ref, w_ref, out_ref):
    out_ref[...] = (part_ref[...] + half_dot(x_ref, w_ref, 1 - lax.axis_index("loop"))).astype(BF16)


def plain_up_kernel(x_ref, w_ref, out_ref):
    out_ref[...] = silu(jnp.dot(x_ref[...], w_ref[0], preferred_element_type=F32)).astype(BF16)


def plain_down_kernel(x_ref, w_ref, out_ref):
    out_ref[...] = jnp.dot(x_ref[...], w_ref[0], preferred_element_type=F32).astype(BF16)


def silu(v):
    return v / (1.0 + jnp.exp(-v))


def on_device(tokens, expert_ids, route_weights, up_proj, down_proj):
    tok_rows, width = tokens.shape
    capacity = tok_rows // 16
    owners = lax.axis_size("expert")
    loops = lax.axis_size("loop")
    per_owner = up_proj.shape[0]
    flight = owners * per_owner
    slots = flight * capacity
    ids_t, weights_t = expert_ids.T, route_weights.T

    outgoing, mix = dispatch(ids_t, weights_t, tokens, flight, capacity)
    arrived = lax.all_to_all(
        outgoing.reshape(owners, per_owner * capacity, width),
        "expert",
        split_axis=0,
        concat_axis=0,
        tiled=True,
    ).reshape(slots, width)

    if loops == 2:
        swap = [(0, 1), (1, 0)]
        theirs = lax.ppermute(arrived, "loop", swap)
        units = up_proj.shape[2]
        part = whole_call(mine_kernel, jax.ShapeDtypeStruct((slots, units), F32), arrived, up_proj)
        hidden = whole_call(up_kernel, jax.ShapeDtypeStruct((slots, units), BF16), part, theirs, up_proj)
        hidden_theirs = lax.ppermute(hidden, "loop", swap)
        part = whole_call(mine_kernel, jax.ShapeDtypeStruct((slots, width), F32), hidden, down_proj)
        out_rows = whole_call(down_kernel, jax.ShapeDtypeStruct((slots, width), BF16), part, hidden_theirs, down_proj)
    else:
        full = lax.all_gather(arrived, "loop", axis=1, tiled=True)
        hidden = whole_call(plain_up_kernel, jax.ShapeDtypeStruct((slots, up_proj.shape[2]), BF16), full, up_proj)
        hidden = lax.all_gather(hidden, "loop", axis=1, tiled=True)
        out_rows = whole_call(plain_down_kernel, jax.ShapeDtypeStruct((slots, width), BF16), hidden, down_proj)

    returned = lax.all_to_all(
        out_rows.reshape(owners, per_owner * capacity, width),
        "expert",
        split_axis=0,
        concat_axis=0,
        tiled=True,
    ).reshape(slots, width)
    return combine(mix, returned)


def solution(mesh):
    return jax.shard_map(
        on_device,
        mesh=mesh,
        in_specs=(
            P("expert", "loop"),
            P("expert", None),
            P("expert", None),
            P("expert", None, "loop"),
            P("expert", None, "loop"),
        ),
        out_specs=P("expert", "loop"),
        check_vma=False,
    )
```

time: 69.6 us -> 68.2 us (0.980)
  local copies, waits for them, and re-layouts: 1.89 us -> 0.02 us
    unnamed x14 -> x6, local copies, waits for them, and re-layouts: 1.89 us -> 0.02 us
    pallas_call x2 -> x3, Pallas kernels: 2.49 us -> 2.96 us  [the longest x1 1.34 us: combine(): pl.pallas_call(combine_kernel, in_specs=[vmem, vmem], out_specs=pl.BlockS...]
where the time goes in v3:
time: 68.2 us; the launch traced here: 68 us
  blocking collectives  59.8 us (88%)
  Pallas kernels  5.58 us (8%)
  waiting for transfers between devices  2.35 us (3%)
    all_to_all x1, blocking collectives, on_device(): lax.all_to_all(outgoing.reshape(owners, per_owner * capacity, width), 'ex...  32.2 us
    all_to_all x1, blocking collectives, on_device(): lax.all_to_all(out_rows.reshape(owners, per_owner * capacity, width), 'ex...  27.6 us
    pallas_call x4, Pallas kernels, whole_call(): pl.pallas_call(kernel, in_specs=[pl.BlockSpec(memory_space=pltpu.VMEM)] *...  2.62 us
    ppermute x1, waiting for transfers between devices, on_device(): theirs = lax.ppermute(arrived, 'loop', swap)  1.8 us
  transfers between devices with their start and end apart: 2, of which 2 were waited for; matrix products, arithmetic and copies ran while one was open for 0% of the time, Pallas kernels for 2%

profile of v3, /device:TPU:0, one launch (start us, length us, event | category | flops | bytes accessed | tf_op | source)
XLA Modules:
  0.0 68.0 jit_solution(13320964386195257791)
XLA Ops:
  0.0 1.2 %shard_map.55 = (bf16[128,3584]{1,0:T(8,128)(2,1)S(1)}, bf16[128,128]{1,0:T(8,128)(2,1)S(1)}, bf16[2,128,128]{2,1,0:T(8,128)(2,1)S(1)}) custom-call(s32[8,128]{1,0:T(8,128)} %bitcast.13, f32[8,128]{1,0:T(8,128)} %bitcast.14, bf16[128,3584]{1,0:T(8,128)(2,1)} %refs_2_.1), custom_call_target="tpu_custom_call" | custom-call | tf_op jit(solution)/shard_map/pallas_call | solution.py:67
  1.2 0.0 copy-start
  1.3 0.4 shard_map.56
  1.6 32.2 %all_to_all.10 = bf16[16,8,3584]{2,1,0:T(8,128)(2,1)S(1)} all-to-all(bf16[16,8,3584]{2,1,0:T(8,128)(2,1)S(1)} %bitcast.12), channel_id=1, replica_groups=mesh['expert'=16,'loop'=2] {'expert'}, dimensions={0} | all-to-all | bytes 1835008 | tf_op jit(solution)/shard_map/all_to_all | solution.py:176
  33.8 0.0 slice-start
  33.8 0.0 collective-permute-start
  33.9 0.0 copy-done
  33.9 0.6 shard_map.57.part_ref
  34.5 0.0 slice-start.1
  34.5 1.8 %collective-permute-done.x_ref = bf16[128,3584]{1,0:T(8,128)(2,1)S(1)} collective-permute-done((bf16[128,3584]{1,0:T(8,128)(2,1)S(1)}, bf16[128,3584]{1,0:T(8,128)(2,1)S(1)}, u32[]{:S(2)}, u32[]{:S(2)}) %collective-permute-start) | collective-permute-done | bytes 917536 | tf_op jit(solution)/shard_map/ppermute | solution.py:186
  36.3 0.7 %shard_map.58.x_ref = bf16[128,512]{1,0:T(8,128)(2,1)S(1)} custom-call(f32[128,512]{1,0:T(8,128)S(1)} %shard_map.57.part_ref, bf16[128,3584]{1,0:T(8,128)(2,1)S(1)} %collective-permute-done.x_ref, bf16[1,7168,512]{2,1,0:T(8,128)(2,1)S(1)} %copy-done), custom_call_target="tpu_custom_call" | custom-call | flops 536870912 | tf_op jit(solution)/shard_map/pallas_call | solution.py:125
  37.0 0.2 collective-permute-start.1
  37.2 0.0 slice-done
  37.2 0.0 slice-done.1
  37.2 0.6 shard_map.59.part_ref
  37.9 0.6 collective-permute-done.1.x_ref
  38.4 0.6 shard_map.60
  39.1 27.6 %all_to_all.11 = bf16[16,8,3584]{2,1,0:T(8,128)(2,1)S(1)} all-to-all(bf16[16,8,3584]{2,1,0:T(8,128)(2,1)S(1)} %bitcast.10), channel_id=1, replica_groups=mesh['expert'=16,'loop'=2] {'expert'}, dimensions={0} | all-to-all | bytes 1835008 | tf_op jit(solution)/shard_map/all_to_all | solution.py:199
  66.7 1.3 %shard_map.61 = bf16[128,3584]{1,0:T(8,128)(2,1)} custom-call(bf16[2,128,128]{2,1,0:T(8,128)(2,1)S(1)} %get-tuple-element.8.mix_ref, bf16[128,3584]{1,0:T(8,128)(2,1)S(1)} %bitcast.11), custom_call_target="tpu_custom_call" | custom-call | tf_op jit(solution)/shard_map/pallas_call | solution.py:111
  (1 shorter events, 0.0 us)
Async XLA Ops:
  1.2 32.6 %copy-start = (bf16[1,7168,512]{2,1,0:T(8,128)(2,1)S(1)}, bf16[1,7168,512]{2,1,0:T(8,128)(2,1)}, u32[]{:S(2)}) copy-start(bf16[1,7168,512]{2,1,0:T(8,128)(2,1)} %w_ref.5) | copy-start | bytes 22020100
  33.8 3.4 %slice-start = ((s8[7340032]{0:T(1024)(128)(4,1)}), s8[4194304]{0:T(1024)(128)(4,1)S(1)}, s32[]{:S(2)}) async-start(s8[7340032]{0:T(1024)(128)(4,1)} %bitcast.6), calls=%async_computation.2 | async-start | bytes 8388608
  33.8 2.5 %collective-permute-start = (bf16[128,3584]{1,0:T(8,128)(2,1)S(1)}, bf16[128,3584]{1,0:T(8,128)(2,1)S(1)}, u32[]{:S(2)}, u32[]{:S(2)}) collective-permute-start(bf16[128,3584]{1,0:T(8,128)(2,1)S(1)} %bitcast.8), channel_id=1, source_target_pairs={{0,1},{1,0},{2,3},{3,2},{4,5},{5,4},{6,7},{7,6},{8,9},{9,8},{10,11... | collective-permute-start | bytes 2752520 | tf_op jit(solution)/shard_map/ppermute | solution.py:186
  34.5 2.7 %slice-start.1 = ((s8[7340032]{0:T(1024)(128)(4,1)}), s8[3145728]{0:T(1024)(128)(4,1)S(1)}, s32[]{:S(2)}) async-start(s8[7340032]{0:T(1024)(128)(4,1)} %bitcast.6), calls=%async_computation.3 | async-start | bytes 6291456
  37.0 1.4 %collective-permute-start.1 = (bf16[128,512]{1,0:T(8,128)(2,1)S(1)}, bf16[128,512]{1,0:T(8,128)(2,1)S(1)}, u32[]{:S(2)}, u32[]{:S(2)}) collective-permute-start(bf16[128,512]{1,0:T(8,128)(2,1)S(1)} %shard_map.58.x_ref), channel_id=1, source_target_pairs={{0,1},{1,0},{2,3},{3,2},{4,5},{5,4},{6,7},{7,6},{8,9},{9,8},{10,11... | collective-permute-start | bytes 393224 | tf_op jit(solution)/shard_map/ppermute | solution.py:190

commit v4 on v3

--- a/solution.py
+++ b/solution.py
@@ -57,10 +57,14 @@
 
 
 def pick_kernel(onehot_ref, held_ref, out_ref):
-    out_ref[...] = jnp.dot(onehot_ref[...], held_ref[...], preferred_element_type=F32).astype(BF16)
-
-
-def dispatch(ids_t, weights_t, tokens, flight, capacity):
+    owners, cores, rows, block = out_ref.shape
+    for core in range(cores):
+        part = held_ref[:, core * block : (core + 1) * block]
+        picked = jnp.dot(onehot_ref[...], part, preferred_element_type=F32).astype(BF16)
+        out_ref[:, core] = picked.reshape(owners, rows, block)
+
+
+def dispatch(ids_t, weights_t, tokens, flight, capacity, shape):
     hbm = pl.BlockSpec(memory_space=pltpu.HBM)
     vmem = pl.BlockSpec(memory_space=pltpu.VMEM)
     slots, tok = flight * capacity, tokens.shape[0]
@@ -85,7 +89,7 @@
         pick_kernel,
         in_specs=[vmem, vmem],
         out_specs=vmem,
-        out_shape=jax.ShapeDtypeStruct((slots, tokens.shape[1]), BF16),
+        out_shape=jax.ShapeDtypeStruct(shape, BF16),
         cost_estimate=pl.CostEstimate(flops=10**11, bytes_accessed=10**8, transcendentals=0),
         compiler_params=pltpu.CompilerParams(vmem_limit_bytes=16 * 2**20),
     )(onehot, held)
@@ -132,22 +136,36 @@
     )(*arrays)
 
 
-def half_dot(x_ref, w_ref, core):
-    depth = x_ref.shape[1]
-    rows = pl.ds(pl.multiple_of(core * depth, depth), depth)
-    return jnp.dot(x_ref[...], w_ref[0, rows, :], preferred_element_type=F32)
-
-
-def mine_kernel(x_ref, w_ref, out_ref):
-    out_ref[...] = half_dot(x_ref, w_ref, lax.axis_index("loop"))
-
-
-def up_kernel(part_ref, x_ref, w_ref, out_ref):
-    out_ref[...] = silu(part_ref[...] + half_dot(x_ref, w_ref, 1 - lax.axis_index("loop"))).astype(BF16)
-
-
-def down_kernel(part_ref, x_ref, w_ref, out_ref):
-    out_ref[...] = (part_ref[...] + half_dot(x_ref, w_ref, 1 - lax.axis_index("loop"))).astype(BF16)
+def up_kernel(x_ref, w_ref, out_ref):
+    owners, cores, rows, block = x_ref.shape
+    me = lax.axis_index("loop")
+    total = None
+    for source in range(cores):
+        x = x_ref[:, source].reshape(owners * rows, block)
+        at = pl.ds(pl.multiple_of((source * cores + me) * block, block), block)
+        term = jnp.dot(x, w_ref[0, at, :], preferred_element_type=F32)
+        total = term if total is None else total + term
+    out_ref[...] = total
+
+
+def up_first_kernel(x_ref, w_ref, up_ref, down_ref, out_ref):
+    up_kernel(x_ref, w_ref, out_ref)
+
+
+def down_dot(part_ref, other_ref, w_ref, core):
+    units = part_ref.shape[1]
+    hidden = silu(part_ref[...] + other_ref[...]).astype(BF16)
+    at = pl.ds(pl.multiple_of(core * units, units), units)
+    return jnp.dot(hidden, w_ref[0, at, :], preferred_element_type=F32)
+
+
+def down_mine_kernel(part_ref, other_ref, w_ref, out_ref):
+    out_ref[...] = down_dot(part_ref, other_ref, w_ref, lax.axis_index("loop"))
+
+
+def down_theirs_kernel(half_ref, part_ref, other_ref, w_ref, out_ref):
+    rest = down_dot(part_ref, other_ref, w_ref, 1 - lax.axis_index("loop"))
+    out_ref[...] = (half_ref[...] + rest).astype(BF16)
 
 
 def plain_up_kernel(x_ref, w_ref, out_ref):
@@ -172,29 +190,56 @@
     slots = flight * capacity
     ids_t, weights_t = expert_ids.T, route_weights.T
 
-    outgoing, mix = dispatch(ids_t, weights_t, tokens, flight, capacity)
-    arrived = lax.all_to_all(
-        outgoing.reshape(owners, per_owner * capacity, width),
-        "expert",
-        split_axis=0,
-        concat_axis=0,
-        tiled=True,
-    ).reshape(slots, width)
-
     if loops == 2:
+        block = width // 2
         swap = [(0, 1), (1, 0)]
-        theirs = lax.ppermute(arrived, "loop", swap)
+        up_theirs = lax.ppermute(up_proj, "loop", swap)
+        outgoing, mix = dispatch(
+            ids_t, weights_t, tokens, flight, capacity, (owners, 2, per_owner * capacity, block)
+        )
+        arrived = lax.all_to_all(
+            outgoing.reshape(owners * 2, per_owner * capacity, block),
+            ("expert", "loop"),
+            split_axis=0,
+            concat_axis=0,
+            tiled=True,
+        ).reshape(outgoing.shape)
         units = up_proj.shape[2]
-        part = whole_call(mine_kernel, jax.ShapeDtypeStruct((slots, units), F32), arrived, up_proj)
-        hidden = whole_call(up_kernel, jax.ShapeDtypeStruct((slots, units), BF16), part, theirs, up_proj)
-        hidden_theirs = lax.ppermute(hidden, "loop", swap)
-        part = whole_call(mine_kernel, jax.ShapeDtypeStruct((slots, width), F32), hidden, down_proj)
-        out_rows = whole_call(down_kernel, jax.ShapeDtypeStruct((slots, width), BF16), part, hidden_theirs, down_proj)
+        sums = jax.ShapeDtypeStruct((slots, units), F32)
+        part_theirs = whole_call(up_first_kernel, sums, arrived, up_theirs, up_proj, down_proj)
+        for_mine = lax.ppermute(part_theirs, "loop", swap)
+        part_mine = whole_call(up_kernel, sums, arrived, up_proj)
+        for_theirs = lax.ppermute(part_mine, "loop", swap)
+        half = whole_call(
+            down_mine_kernel, jax.ShapeDtypeStruct((slots, width), F32), part_mine, for_mine, down_proj
+        )
+        out_rows = whole_call(
+            down_theirs_kernel,
+            jax.ShapeDtypeStruct((slots, width), BF16),
+            half,
+            part_theirs,
+            for_theirs,
+            down_proj,
+        )
     else:
+        outgoing, mix = dispatch(
+            ids_t, weights_t, tokens, flight, capacity, (owners, 1, per_owner * capacity, width)
+        )
+        arrived = lax.all_to_all(
+            outgoing.reshape(owners, per_owner * capacity, width),
+            "expert",
+            split_axis=0,
+            concat_axis=0,
+            tiled=True,
+        ).reshape(slots, width)
         full = lax.all_gather(arrived, "loop", axis=1, tiled=True)
-        hidden = whole_call(plain_up_kernel, jax.ShapeDtypeStruct((slots, up_proj.shape[2]), BF16), full, up_proj)
+        hidden = whole_call(
+            plain_up_kernel, jax.ShapeDtypeStruct((slots, up_proj.shape[2]), BF16), full, up_proj
+        )
         hidden = lax.all_gather(hidden, "loop", axis=1, tiled=True)
-        out_rows = whole_call(plain_down_kernel, jax.ShapeDtypeStruct((slots, width), BF16), hidden, down_proj)
+        out_rows = whole_call(
+            plain_down_kernel, jax.ShapeDtypeStruct((slots, width), BF16), hidden, down_proj
+        )
 
     returned = lax.all_to_all(
         out_rows.reshape(owners, per_owner * capacity, width),

time: 68.2 us -> 66.5 us (0.975)
  waiting for transfers between devices: 2.35 us -> 0.5 us
  starting transfers between devices: 0.21 us -> 1.08 us
  blocking collectives: 59.8 us -> 59 us
    all_to_all x1, blocking collectives: 32.2 us -> 30.2 us  [on_device(): lax.all_to_all(outgoing.reshape(owners * 2, per_owner * capacity, block),...]
    ppermute x2 -> x3, waiting for transfers between devices: 2.35 us -> 0.5 us  [the longest x1 0.32 us: on_device(): for_mine = lax.ppermute(part_theirs, 'loop', swap)]
    all_to_all x1, blocking collectives: 27.6 us -> 28.8 us  [on_device(): lax.all_to_all(out_rows.reshape(owners, per_owner * capacity, width), 'ex...]
    ppermute x2 -> x3, starting transfers between devices: 0.21 us -> 1.08 us  [the longest x1 0.55 us: on_device(): for_theirs = lax.ppermute(part_mine, 'loop', swap)]
  transfers between devices with their start and end apart: 2 -> 3, of which waited for: 2 -> 2; matrix products, arithmetic and copies ran while one was open for 0% -> 0% of each run, Pallas kernels for 2% -> 4%
where the time goes in v4:
time: 66.5 us; the launch traced here: 66.2 us
  blocking collectives  59 us (89%)
  Pallas kernels  5.57 us (8%)
  starting transfers between devices  1.08 us (2%)
    all_to_all x1, blocking collectives, on_device(): lax.all_to_all(outgoing.reshape(owners * 2, per_owner * capacity, block),...  30.2 us
    all_to_all x1, blocking collectives, on_device(): lax.all_to_all(out_rows.reshape(owners, per_owner * capacity, width), 'ex...  28.8 us
    pallas_call x4, Pallas kernels, whole_call(): pl.pallas_call(kernel, in_specs=[pl.BlockSpec(memory_space=pltpu.VMEM)] *...  2.61 us
    pallas_call x1, Pallas kernels, combine(): pl.pallas_call(combine_kernel, in_specs=[vmem, vmem], out_specs=pl.BlockS...  1.34 us
  transfers between devices with their start and end apart: 3, of which 2 were waited for; matrix products, arithmetic and copies ran while one was open for 0% of the time, Pallas kernels for 4%

profile of v4, /device:TPU:0, one launch (start us, length us, event | category | flops | bytes accessed | tf_op | source)
XLA Modules:
  0.0 66.2 jit_solution(13731219279254590804)
XLA Ops:
  0.0 0.5 collective-permute-start
  0.5 1.2 %shard_map.55 = (bf16[128,3584]{1,0:T(8,128)(2,1)S(1)}, bf16[128,128]{1,0:T(8,128)(2,1)S(1)}, bf16[2,128,128]{2,1,0:T(8,128)(2,1)S(1)}) custom-call(s32[8,128]{1,0:T(8,128)} %bitcast.11, f32[8,128]{1,0:T(8,128)} %bitcast.12, bf16[128,3584]{1,0:T(8,128)(2,1)} %refs_2_.1), custom_call_target="tpu_custom_call" | custom-call | tf_op jit(solution)/shard_map/pallas_call | solution.py:71
  1.7 0.0 copy-start
  1.7 0.0 copy-start.1
  1.7 0.4 shard_map.56
  2.1 30.2 %all_to_all.10 = bf16[32,8,1792]{2,1,0:T(8,128)(2,1)S(1)} all-to-all(bf16[32,8,1792]{2,1,0:T(8,128)(2,1)S(1)} %bitcast.10), channel_id=1, replica_groups=mesh['expert'=16,'loop'=2] {'expert','loop'}, dimensions={0} | all-to-all | bytes 1835008 | tf_op jit(solution)/shard_map/all_to_all | solution.py:200
  32.3 0.0 collective-permute-done.w_ref
  32.3 0.0 copy-done
  32.3 0.0 copy-done.1
  32.3 0.7 shard_map.58.part_ref
  33.0 0.1 collective-permute-start.1
  33.1 0.6 shard_map.57.part_ref
  33.7 0.6 collective-permute-start.2
  34.3 0.3 collective-permute-done.1.other_ref
  34.6 0.7 shard_map.59.half_ref
  35.2 0.2 collective-permute-done.2.other_ref
  35.4 0.7 shard_map.60
  36.1 28.8 %all_to_all.11 = bf16[16,8,3584]{2,1,0:T(8,128)(2,1)S(1)} all-to-all(bf16[16,8,3584]{2,1,0:T(8,128)(2,1)S(1)} %bitcast.9), channel_id=1, replica_groups=mesh['expert'=16,'loop'=2] {'expert'}, dimensions={0} | all-to-all | bytes 1835008 | tf_op jit(solution)/shard_map/all_to_all | solution.py:244
  64.9 1.3 %shard_map.61 = bf16[128,3584]{1,0:T(8,128)(2,1)} custom-call(bf16[2,128,128]{2,1,0:T(8,128)(2,1)S(1)} %get-tuple-element.8.mix_ref, bf16[128,3584]{1,0:T(8,128)(2,1)S(1)} %bitcast.8), custom_call_target="tpu_custom_call" | custom-call | tf_op jit(solution)/shard_map/pallas_call | solution.py:115
Async XLA Ops:
  0.0 32.3 %collective-permute-start = (bf16[1,7168,512]{2,1,0:T(8,128)(2,1)}, bf16[1,7168,512]{2,1,0:T(8,128)(2,1)S(1)}, u32[]{:S(2)}, u32[]{:S(2)}) collective-permute-start(bf16[1,7168,512]{2,1,0:T(8,128)(2,1)} %up_ref.1), channel_id=1, source_target_pairs={{0,1},{1,0},{2,3},{3,2},{4,5},{5,4},{6,7},{7,6},{8,9},{9,8},{10,11... | collective-permute-start | bytes 22020104 | tf_op jit(solution)/shard_map/ppermute | solution.py:196
  1.7 30.6 %copy-start = (bf16[1,1024,3584]{2,1,0:T(8,128)(2,1)S(1)}, bf16[1,1024,3584]{2,1,0:T(8,128)(2,1)}, u32[]{:S(2)}) copy-start(bf16[1,1024,3584]{2,1,0:T(8,128)(2,1)} %w_ref.5) | copy-start | bytes 22020100
  1.7 30.6 %copy-start.1 = (bf16[1,7168,512]{2,1,0:T(8,128)(2,1)S(1)}, bf16[1,7168,512]{2,1,0:T(8,128)(2,1)}, u32[]{:S(2)}) copy-start(bf16[1,7168,512]{2,1,0:T(8,128)(2,1)} %up_ref.1) | copy-start | bytes 22020100
  33.0 1.6 %collective-permute-start.1 = (f32[128,512]{1,0:T(8,128)S(1)}, f32[128,512]{1,0:T(8,128)S(1)}, u32[]{:S(2)}, u32[]{:S(2)}) collective-permute-start(f32[128,512]{1,0:T(8,128)S(1)} %shard_map.58.part_ref), channel_id=1, source_target_pairs={{0,1},{1,0},{2,3},{3,2},{4,5},{5,4},{6,7},{7,6},{8,9},{9,8},{10,11... | collective-permute-start | bytes 786440 | tf_op jit(solution)/shard_map/ppermute | solution.py:210
  33.7 1.7 %collective-permute-start.2 = (f32[128,512]{1,0:T(8,128)S(1)}, f32[128,512]{1,0:T(8,128)S(1)}, u32[]{:S(2)}, u32[]{:S(2)}) collective-permute-start(f32[128,512]{1,0:T(8,128)S(1)} %shard_map.57.part_ref), channel_id=1, source_target_pairs={{0,1},{1,0},{2,3},{3,2},{4,5},{5,4},{6,7},{7,6},{8,9},{9,8},{10,11... | collective-permute-start | bytes 786440 | tf_op jit(solution)/shard_map/ppermute | solution.py:212

commit v5 on v4

--- a/solution.py
+++ b/solution.py
@@ -7,9 +7,15 @@
 
 BF16, F32 = jnp.bfloat16, jnp.float32
 COMBINE_BLOCKS, MIX_PARTS = 7, 2
-
-
-def slot_tables(ids_ref, weights_ref, onehot_ref, mix_ref, flight, capacity):
+DISPATCH_ORDER = [11, 15, 9, 13, 3, 7, 1, 5, 10, 14, 8, 12, 2, 6, 0, 4]
+RETURN_ORDER = [11, 3, 10, 2, 9, 1, 8, 0, 15, 7, 14, 6, 13, 5, 12, 4]
+
+
+def reorder(rows, order, size):
+    return jnp.concatenate([rows[i * size : (i + 1) * size] for i in order], axis=0)
+
+
+def slot_tables(ids_ref, weights_ref, onehot_ref, mix_ref, flight, capacity, orders):
     top, tok = ids_ref.shape
     experts = lax.broadcasted_iota(jnp.int32, (flight, tok), 0)
     chosen = jnp.zeros((flight, tok), F32)
@@ -27,11 +33,17 @@
     rank = jnp.where(chosen > 0.5, rank, -1.0)
     places = lax.broadcasted_iota(jnp.int32, (flight, capacity, tok), 1).astype(F32)
     picked = rank[:, None, :] == places
-    onehot_ref[...] = jnp.where(picked, 1.0, 0.0).reshape(flight * capacity, tok).astype(BF16)
-    mix = jnp.where(picked, weight[:, None, :], 0.0).reshape(flight * capacity, tok).T
+    onehot = jnp.where(picked, 1.0, 0.0).reshape(flight * capacity, tok)
+    mix = jnp.where(picked, weight[:, None, :], 0.0).reshape(flight * capacity, tok)
+    if orders is not None:
+        onehot = reorder(onehot, orders[0], capacity)
+        mix = reorder(mix, orders[1], capacity)
+    onehot_ref[...] = onehot.astype(BF16)
+    mix = mix.T
+    slots = flight * capacity
     for i in range(MIX_PARTS):
         part = mix.astype(BF16)
-        mix_ref[i] = part
+        mix_ref[:, i * slots : (i + 1) * slots] = part
         mix = mix - part.astype(F32)
 
 
@@ -41,7 +53,7 @@
 
 
 def read_kernel(
-    flight, capacity, ids_ref, weights_ref, tokens_ref, held, onehot_ref, mix_ref, ids, weights, sems
+    flight, capacity, orders, ids_ref, weights_ref, tokens_ref, held, onehot_ref, mix_ref, ids, weights, sems
 ):
     copies = [
         pltpu.make_async_copy(ids_ref, ids, sems.at[0]),
@@ -52,7 +64,7 @@
         copy.start()
     copies[0].wait()
     copies[1].wait()
-    slot_tables(ids, weights, onehot_ref, mix_ref, flight, capacity)
+    slot_tables(ids, weights, onehot_ref, mix_ref, flight, capacity, orders)
     copies[2].wait()
 
 
@@ -64,18 +76,18 @@
         out_ref[:, core] = picked.reshape(owners, rows, block)
 
 
-def dispatch(ids_t, weights_t, tokens, flight, capacity, shape):
+def dispatch(ids_t, weights_t, tokens, flight, capacity, shape, orders):
     hbm = pl.BlockSpec(memory_space=pltpu.HBM)
     vmem = pl.BlockSpec(memory_space=pltpu.VMEM)
     slots, tok = flight * capacity, tokens.shape[0]
     held, onehot, mix = pl.pallas_call(
-        lambda *refs: read_kernel(flight, capacity, *refs),
+        lambda *refs: read_kernel(flight, capacity, orders, *refs),
         in_specs=[hbm, hbm, hbm],
         out_specs=[vmem, vmem, vmem],
         out_shape=[
             jax.ShapeDtypeStruct(tokens.shape, BF16),
             jax.ShapeDtypeStruct((slots, tok), BF16),
-            jax.ShapeDtypeStruct((MIX_PARTS, tok, slots), BF16),
+            jax.ShapeDtypeStruct((tok, MIX_PARTS * slots), BF16),
         ],
         scratch_shapes=[
             pltpu.VMEM(ids_t.shape, jnp.int32),
@@ -99,10 +111,8 @@
 def combine_kernel(mix_ref, rows_ref, out_ref, held, sems):
     copies = []
     for i, at in enumerate(column_blocks(held.shape[1], COMBINE_BLOCKS)):
-        rows = rows_ref[:, at]
-        held[:, at] = sum(
-            jnp.dot(mix_ref[k], rows, preferred_element_type=F32) for k in range(MIX_PARTS)
-        ).astype(BF16)
+        rows = jnp.concatenate([rows_ref[:, at]] * MIX_PARTS, axis=0)
+        held[:, at] = jnp.dot(mix_ref[...], rows, preferred_element_type=F32).astype(BF16)
         copies.append(pltpu.make_async_copy(held.at[:, at], out_ref.at[:, at], sems.at[i]))
         copies[-1].start()
     for copy in copies:
@@ -110,7 +120,7 @@
 
 
 def combine(mix, rows):
-    tok, width = mix.shape[1], rows.shape[1]
+    tok, width = mix.shape[0], rows.shape[1]
     vmem = pl.BlockSpec(memory_space=pltpu.VMEM)
     return pl.pallas_call(
         combine_kernel,
@@ -152,19 +162,22 @@
     up_kernel(x_ref, w_ref, out_ref)
 
 
-def down_dot(part_ref, other_ref, w_ref, core):
+def down_dot(back, part_ref, other_ref, w_ref, core):
     units = part_ref.shape[1]
-    hidden = silu(part_ref[...] + other_ref[...]).astype(BF16)
+    sums = part_ref[...] + other_ref[...]
+    if back is not None:
+        sums = reorder(sums, back, sums.shape[0] // len(back))
+    hidden = silu(sums).astype(BF16)
     at = pl.ds(pl.multiple_of(core * units, units), units)
     return jnp.dot(hidden, w_ref[0, at, :], preferred_element_type=F32)
 
 
-def down_mine_kernel(part_ref, other_ref, w_ref, out_ref):
-    out_ref[...] = down_dot(part_ref, other_ref, w_ref, lax.axis_index("loop"))
-
-
-def down_theirs_kernel(half_ref, part_ref, other_ref, w_ref, out_ref):
-    rest = down_dot(part_ref, other_ref, w_ref, 1 - lax.axis_index("loop"))
+def down_mine_kernel(back, part_ref, other_ref, w_ref, out_ref):
+    out_ref[...] = down_dot(back, part_ref, other_ref, w_ref, lax.axis_index("loop"))
+
+
+def down_theirs_kernel(back, half_ref, part_ref, other_ref, w_ref, out_ref):
+    rest = down_dot(back, part_ref, other_ref, w_ref, 1 - lax.axis_index("loop"))
     out_ref[...] = (half_ref[...] + rest).astype(BF16)
 
 
@@ -190,18 +203,26 @@
     slots = flight * capacity
     ids_t, weights_t = expert_ids.T, route_weights.T
 
+    orders = back = pairs = singles = None
+    if loops == 2 and owners == len(DISPATCH_ORDER) and per_owner == 1:
+        orders = (DISPATCH_ORDER, RETURN_ORDER)
+        back = [DISPATCH_ORDER.index(owner) for owner in RETURN_ORDER]
+        pairs = [[owner * 2 + core for owner in DISPATCH_ORDER for core in range(2)]]
+        singles = [RETURN_ORDER]
+
     if loops == 2:
         block = width // 2
         swap = [(0, 1), (1, 0)]
         up_theirs = lax.ppermute(up_proj, "loop", swap)
         outgoing, mix = dispatch(
-            ids_t, weights_t, tokens, flight, capacity, (owners, 2, per_owner * capacity, block)
+            ids_t, weights_t, tokens, flight, capacity, (owners, 2, per_owner * capacity, block), orders
         )
         arrived = lax.all_to_all(
             outgoing.reshape(owners * 2, per_owner * capacity, block),
             ("expert", "loop"),
             split_axis=0,
             concat_axis=0,
+            axis_index_groups=pairs,
             tiled=True,
         ).reshape(outgoing.shape)
         units = up_proj.shape[2]
@@ -211,10 +232,14 @@
         part_mine = whole_call(up_kernel, sums, arrived, up_proj)
         for_theirs = lax.ppermute(part_mine, "loop", swap)
         half = whole_call(
-            down_mine_kernel, jax.ShapeDtypeStruct((slots, width), F32), part_mine, for_mine, down_proj
+            lambda *refs: down_mine_kernel(back, *refs),
+            jax.ShapeDtypeStruct((slots, width), F32),
+            part_mine,
+            for_mine,
+            down_proj,
         )
         out_rows = whole_call(
-            down_theirs_kernel,
+            lambda *refs: down_theirs_kernel(back, *refs),
             jax.ShapeDtypeStruct((slots, width), BF16),
             half,
             part_theirs,
@@ -223,7 +248,7 @@
         )
     else:
         outgoing, mix = dispatch(
-            ids_t, weights_t, tokens, flight, capacity, (owners, 1, per_owner * capacity, width)
+            ids_t, weights_t, tokens, flight, capacity, (owners, 1, per_owner * capacity, width), None
         )
         arrived = lax.all_to_all(
             outgoing.reshape(owners, per_owner * capacity, width),
@@ -246,6 +271,7 @@
         "expert",
         split_axis=0,
         concat_axis=0,
+        axis_index_groups=singles,
         tiled=True,
     ).reshape(slots, width)
     return combine(mix, returned)

time: 66.5 us -> 63.3 us (0.952)
  blocking collectives: 59 us -> 55.8 us
    all_to_all x1, blocking collectives: 28.8 us -> 25.9 us  [on_device(): lax.all_to_all(out_rows.reshape(owners, per_owner * capacity, width), 'ex...]
  transfers between devices with their start and end apart: 3 -> 3, of which waited for: 2 -> 2; matrix products, arithmetic and copies ran while one was open for 0% -> 0% of each run, Pallas kernels for 4% -> 5%
where the time goes in v5:
time: 63.3 us; the launch traced here: 63 us
  blocking collectives  55.8 us (88%)
  Pallas kernels  5.4 us (9%)
  starting transfers between devices  1.1 us (2%)
  waiting for transfers between devices  0.64 us (1%)
    all_to_all x1, blocking collectives, on_device(): lax.all_to_all(outgoing.reshape(owners * 2, per_owner * capacity, block),...  29.9 us
    all_to_all x1, blocking collectives, on_device(): lax.all_to_all(out_rows.reshape(owners, per_owner * capacity, width), 'ex...  25.9 us
    pallas_call x4, Pallas kernels, whole_call(): pl.pallas_call(kernel, in_specs=[pl.BlockSpec(memory_space=pltpu.VMEM)] *...  2.6 us
  transfers between devices with their start and end apart: 3, of which 2 were waited for; matrix products, arithmetic and copies ran while one was open for 0% of the time, Pallas kernels for 5%

profile of v5, /device:TPU:0, one launch (start us, length us, event | category | flops | bytes accessed | tf_op | source)
XLA Modules:
  0.0 63.0 jit_solution(2264853373758624818)
XLA Ops:
  0.0 0.5 collective-permute-start
  0.5 1.2 %shard_map.55 = (bf16[128,3584]{1,0:T(8,128)(2,1)S(1)}, bf16[128,128]{1,0:T(8,128)(2,1)S(1)}, bf16[128,256]{1,0:T(8,128)(2,1)S(1)}) custom-call(s32[8,128]{1,0:T(8,128)} %bitcast.11, f32[8,128]{1,0:T(8,128)} %bitcast.12, bf16[128,3584]{1,0:T(8,128)(2,1)} %refs_2_.2), custom_call_target="tpu_custom_call" | custom-call | tf_op jit(solution)/shard_map/pallas_call | solution.py:83
  1.7 0.0 copy-start
  1.7 0.0 copy-start.1
  1.7 0.4 shard_map.56
  2.1 29.9 %all_to_all.10 = bf16[32,8,1792]{2,1,0:T(8,128)(2,1)S(1)} all-to-all(bf16[32,8,1792]{2,1,0:T(8,128)(2,1)S(1)} %bitcast.10), channel_id=1, replica_groups={{22,23,30,31,18,19,26,27,6,7,14,15,2,3,10,11,20,21,28,29,16,17,24,25,4,..., dimensions={0} | all-to-all | bytes 1835008 | tf_op jit(solution)/shard_map/all_to_all | solution.py:220
  32.0 0.0 collective-permute-done.w_ref
  32.0 0.0 copy-done
  32.0 0.0 copy-done.1
  32.0 0.6 %shard_map.58.refs_1_ = f32[128,512]{1,0:T(8,128)S(1)} custom-call(bf16[16,2,8,1792]{3,2,1,0:T(8,128)(2,1)S(1)} %bitcast.6, bf16[1,7168,512]{2,1,0:T(8,128)(2,1)S(1)} %collective-permute-done.w_ref, bf16[1,7168,512]{2,1,0:T(8,128)(2,1)S(1)} %copy-done.1, bf16[1,1024,3584]{2,1,0:T(8,128)(2,1)S(1)} %copy-done), custom_call_target="tpu_custom_call" | custom-call | flops 536870912 | tf_op jit(solution)/shard_map/pallas_call | solution.py:139
  32.7 0.3 collective-permute-start.1
  33.0 0.6 %shard_map.57.refs_0_ = f32[128,512]{1,0:T(8,128)S(1)} custom-call(bf16[16,2,8,1792]{3,2,1,0:T(8,128)(2,1)S(1)} %bitcast.7, bf16[1,7168,512]{2,1,0:T(8,128)(2,1)S(1)} %copy-done.1), custom_call_target="tpu_custom_call" | custom-call | flops 536870912 | tf_op jit(solution)/shard_map/pallas_call | solution.py:139
  33.7 0.3 collective-permute-start.2
  34.0 0.3 collective-permute-done.1.refs_1_
  34.3 0.7 %shard_map.59.refs_0_ = f32[128,3584]{1,0:T(8,128)S(1)} custom-call(f32[128,512]{1,0:T(8,128)S(1)} %shard_map.57.refs_0_, f32[128,512]{1,0:T(8,128)S(1)} %collective-permute-done.1.refs_1_, bf16[1,1024,3584]{2,1,0:T(8,128)(2,1)S(1)} %copy-done), custom_call_target="tpu_custom_call" | custom-call | flops 536870912 | tf_op jit(solution)/shard_map/pallas_call | solution.py:139
  34.9 0.3 collective-permute-done.2.refs_2_
  35.3 0.7 %shard_map.60 = bf16[128,3584]{1,0:T(8,128)(2,1)S(1)} custom-call(f32[128,3584]{1,0:T(8,128)S(1)} %shard_map.59.refs_0_, f32[128,512]{1,0:T(8,128)S(1)} %shard_map.58.refs_1_, f32[128,512]{1,0:T(8,128)S(1)} %collective-permute-done.2.refs_2_, bf16[1,1024,3584]{2,1,0:T(8,128)(2,1)S(1)} %copy-done), custom_call_target="tpu_custom_call" | custom-call | flops 536870912 | tf_op jit(solution)/shard_map/pallas_call | solution.py:139
  35.9 25.9 %all_to_all.11 = bf16[16,8,3584]{2,1,0:T(8,128)(2,1)S(1)} all-to-all(bf16[16,8,3584]{2,1,0:T(8,128)(2,1)S(1)} %bitcast.9), channel_id=1, replica_groups={{22,6,20,4,18,2,16,0,30,14,28,12,26,10,24,8},{23,7,21,5,19,3,17,1,31,15..., dimensions={0} | all-to-all | bytes 1835008 | tf_op jit(solution)/shard_map/all_to_all | solution.py:269
  61.8 1.2 %shard_map.61 = bf16[128,3584]{1,0:T(8,128)(2,1)} custom-call(bf16[128,256]{1,0:T(8,128)(2,1)S(1)} %get-tuple-element.8.mix_ref, bf16[128,3584]{1,0:T(8,128)(2,1)S(1)} %bitcast.8), custom_call_target="tpu_custom_call" | custom-call | tf_op jit(solution)/shard_map/pallas_call | solution.py:125
Async XLA Ops:
  0.0 32.0 %collective-permute-start = (bf16[1,7168,512]{2,1,0:T(8,128)(2,1)}, bf16[1,7168,512]{2,1,0:T(8,128)(2,1)S(1)}, u32[]{:S(2)}, u32[]{:S(2)}) collective-permute-start(bf16[1,7168,512]{2,1,0:T(8,128)(2,1)} %up_ref.1), channel_id=1, source_target_pairs={{0,1},{1,0},{2,3},{3,2},{4,5},{5,4},{6,7},{7,6},{8,9},{9,8},{10,11... | collective-permute-start | bytes 22020104 | tf_op jit(solution)/shard_map/ppermute | solution.py:216
  1.7 30.3 %copy-start = (bf16[1,1024,3584]{2,1,0:T(8,128)(2,1)S(1)}, bf16[1,1024,3584]{2,1,0:T(8,128)(2,1)}, u32[]{:S(2)}) copy-start(bf16[1,1024,3584]{2,1,0:T(8,128)(2,1)} %refs_3_.1) | copy-start | bytes 22020100
  1.7 30.3 %copy-start.1 = (bf16[1,7168,512]{2,1,0:T(8,128)(2,1)S(1)}, bf16[1,7168,512]{2,1,0:T(8,128)(2,1)}, u32[]{:S(2)}) copy-start(bf16[1,7168,512]{2,1,0:T(8,128)(2,1)} %up_ref.1) | copy-start | bytes 22020100
  32.7 1.6 %collective-permute-start.1 = (f32[128,512]{1,0:T(8,128)S(1)}, f32[128,512]{1,0:T(8,128)S(1)}, u32[]{:S(2)}, u32[]{:S(2)}) collective-permute-start(f32[128,512]{1,0:T(8,128)S(1)} %shard_map.58.refs_1_), channel_id=1, source_target_pairs={{0,1},{1,0},{2,3},{3,2},{4,5},{5,4},{6,7},{7,6},{8,9},{9,8},{10,11... | collective-permute-start | bytes 786440 | tf_op jit(solution)/shard_map/ppermute | solution.py:231
  33.7 1.6 %collective-permute-start.2 = (f32[128,512]{1,0:T(8,128)S(1)}, f32[128,512]{1,0:T(8,128)S(1)}, u32[]{:S(2)}, u32[]{:S(2)}) collective-permute-start(f32[128,512]{1,0:T(8,128)S(1)} %shard_map.57.refs_0_), channel_id=1, source_target_pairs={{0,1},{1,0},{2,3},{3,2},{4,5},{5,4},{6,7},{7,6},{8,9},{9,8},{10,11... | collective-permute-start | bytes 786440 | tf_op jit(solution)/shard_map/ppermute | solution.py:233

commit v6 on v5

--- a/solution.py
+++ b/solution.py
@@ -7,7 +7,7 @@
 
 BF16, F32 = jnp.bfloat16, jnp.float32
 COMBINE_BLOCKS, MIX_PARTS = 7, 2
-DISPATCH_ORDER = [11, 15, 9, 13, 3, 7, 1, 5, 10, 14, 8, 12, 2, 6, 0, 4]
+DISPATCH_ORDER = [11, 15, 10, 14, 3, 7, 2, 6, 9, 13, 8, 12, 1, 5, 0, 4]
 RETURN_ORDER = [11, 3, 10, 2, 9, 1, 8, 0, 15, 7, 14, 6, 13, 5, 12, 4]
 
 
@@ -69,11 +69,11 @@
 
 
 def pick_kernel(onehot_ref, held_ref, out_ref):
-    owners, cores, rows, block = out_ref.shape
+    cores, owners, rows, block = out_ref.shape
     for core in range(cores):
         part = held_ref[:, core * block : (core + 1) * block]
         picked = jnp.dot(onehot_ref[...], part, preferred_element_type=F32).astype(BF16)
-        out_ref[:, core] = picked.reshape(owners, rows, block)
+        out_ref[core] = picked.reshape(owners, rows, block)
 
 
 def dispatch(ids_t, weights_t, tokens, flight, capacity, shape, orders):
@@ -147,11 +147,11 @@
 
 
 def up_kernel(x_ref, w_ref, out_ref):
-    owners, cores, rows, block = x_ref.shape
+    cores, owners, rows, block = x_ref.shape
     me = lax.axis_index("loop")
     total = None
     for source in range(cores):
-        x = x_ref[:, source].reshape(owners * rows, block)
+        x = x_ref[source].reshape(owners * rows, block)
         at = pl.ds(pl.multiple_of((source * cores + me) * block, block), block)
         term = jnp.dot(x, w_ref[0, at, :], preferred_element_type=F32)
         total = term if total is None else total + term
@@ -203,11 +203,12 @@
     slots = flight * capacity
     ids_t, weights_t = expert_ids.T, route_weights.T
 
-    orders = back = pairs = singles = None
+    orders = back = singles = None
+    pairs = [[owner * 2 + core for core in range(2) for owner in range(owners)]]
     if loops == 2 and owners == len(DISPATCH_ORDER) and per_owner == 1:
         orders = (DISPATCH_ORDER, RETURN_ORDER)
         back = [DISPATCH_ORDER.index(owner) for owner in RETURN_ORDER]
-        pairs = [[owner * 2 + core for owner in DISPATCH_ORDER for core in range(2)]]
+        pairs = [[owner * 2 + core for core in range(2) for owner in DISPATCH_ORDER]]
         singles = [RETURN_ORDER]
 
     if loops == 2:
@@ -215,7 +216,7 @@
         swap = [(0, 1), (1, 0)]
         up_theirs = lax.ppermute(up_proj, "loop", swap)
         outgoing, mix = dispatch(
-            ids_t, weights_t, tokens, flight, capacity, (owners, 2, per_owner * capacity, block), orders
+            ids_t, weights_t, tokens, flight, capacity, (2, owners, per_owner * capacity, block), orders
         )
         arrived = lax.all_to_all(
             outgoing.reshape(owners * 2, per_owner * capacity, block),
@@ -248,7 +249,7 @@
         )
     else:
         outgoing, mix = dispatch(
-            ids_t, weights_t, tokens, flight, capacity, (owners, 1, per_owner * capacity, width), None
+            ids_t, weights_t, tokens, flight, capacity, (1, owners, per_owner * capacity, width), None
         )
         arrived = lax.all_to_all(
             outgoing.reshape(owners, per_owner * capacity, width),

time: 63.3 us -> 62.6 us (0.989)
    all_to_all x1, blocking collectives: 29.9 us -> 27.4 us  [on_device(): lax.all_to_all(outgoing.reshape(owners * 2, per_owner * capacity, block),...]
    all_to_all x1, blocking collectives: 25.9 us -> 27.8 us  [on_device(): lax.all_to_all(out_rows.reshape(owners, per_owner * capacity, width), 'ex...]
where the time goes in v6:
time: 62.6 us; the launch traced here: 62.3 us
  blocking collectives  55.2 us (88%)
  Pallas kernels  5.4 us (9%)
  starting transfers between devices  1.09 us (2%)
    all_to_all x1, blocking collectives, on_device(): lax.all_to_all(out_rows.reshape(owners, per_owner * capacity, width), 'ex...  27.8 us
    all_to_all x1, blocking collectives, on_device(): lax.all_to_all(outgoing.reshape(owners * 2, per_owner * capacity, block),...  27.4 us
    pallas_call x4, Pallas kernels, whole_call(): pl.pallas_call(kernel, in_specs=[pl.BlockSpec(memory_space=pltpu.VMEM)] *...  2.6 us
  transfers between devices with their start and end apart: 3, of which 2 were waited for; matrix products, arithmetic and copies ran while one was open for 0% of the time, Pallas kernels for 5%

profile of v6, /device:TPU:0, one launch (start us, length us, event | category | flops | bytes accessed | tf_op | source)
XLA Modules:
  0.0 62.3 jit_solution(13699884521297532270)
XLA Ops:
  0.0 0.5 collective-permute-start
  0.5 1.2 %shard_map.55 = (bf16[128,3584]{1,0:T(8,128)(2,1)S(1)}, bf16[128,128]{1,0:T(8,128)(2,1)S(1)}, bf16[128,256]{1,0:T(8,128)(2,1)S(1)}) custom-call(s32[8,128]{1,0:T(8,128)} %bitcast.11, f32[8,128]{1,0:T(8,128)} %bitcast.12, bf16[128,3584]{1,0:T(8,128)(2,1)} %refs_2_.2), custom_call_target="tpu_custom_call" | custom-call | tf_op jit(solution)/shard_map/pallas_call | solution.py:83
  1.7 0.0 copy-start
  1.7 0.0 copy-start.1
  1.7 0.4 shard_map.56
  2.1 27.4 %all_to_all.10 = bf16[32,8,1792]{2,1,0:T(8,128)(2,1)S(1)} all-to-all(bf16[32,8,1792]{2,1,0:T(8,128)(2,1)S(1)} %bitcast.10), channel_id=1, replica_groups={{22,30,20,28,6,14,4,12,18,26,16,24,2,10,0,8,23,31,21,29,7,15,5,13,19,27..., dimensions={0} | all-to-all | bytes 1835008 | tf_op jit(solution)/shard_map/all_to_all | solution.py:221
  29.5 0.0 collective-permute-done.w_ref
  29.5 0.0 copy-done
  29.5 0.0 copy-done.1
  29.5 0.7 %shard_map.58.refs_1_ = f32[128,512]{1,0:T(8,128)S(1)} custom-call(bf16[2,16,8,1792]{3,2,1,0:T(8,128)(2,1)S(1)} %bitcast.6, bf16[1,7168,512]{2,1,0:T(8,128)(2,1)S(1)} %collective-permute-done.w_ref, bf16[1,7168,512]{2,1,0:T(8,128)(2,1)S(1)} %copy-done.1, bf16[1,1024,3584]{2,1,0:T(8,128)(2,1)S(1)} %copy-done), custom_call_target="tpu_custom_call" | custom-call | flops 536870912 | tf_op jit(solution)/shard_map/pallas_call | solution.py:139
  30.1 0.1 collective-permute-start.1
  30.2 0.6 %shard_map.57.refs_0_ = f32[128,512]{1,0:T(8,128)S(1)} custom-call(bf16[2,16,8,1792]{3,2,1,0:T(8,128)(2,1)S(1)} %bitcast.7, bf16[1,7168,512]{2,1,0:T(8,128)(2,1)S(1)} %copy-done.1), custom_call_target="tpu_custom_call" | custom-call | flops 536870912 | tf_op jit(solution)/shard_map/pallas_call | solution.py:139
  30.9 0.5 collective-permute-start.2
  31.4 0.3 collective-permute-done.1.refs_1_
  31.8 0.7 %shard_map.59.refs_0_ = f32[128,3584]{1,0:T(8,128)S(1)} custom-call(f32[128,512]{1,0:T(8,128)S(1)} %shard_map.57.refs_0_, f32[128,512]{1,0:T(8,128)S(1)} %collective-permute-done.1.refs_1_, bf16[1,1024,3584]{2,1,0:T(8,128)(2,1)S(1)} %copy-done), custom_call_target="tpu_custom_call" | custom-call | flops 536870912 | tf_op jit(solution)/shard_map/pallas_call | solution.py:139
  32.4 0.2 collective-permute-done.2.refs_2_
  32.6 0.7 %shard_map.60 = bf16[128,3584]{1,0:T(8,128)(2,1)S(1)} custom-call(f32[128,3584]{1,0:T(8,128)S(1)} %shard_map.59.refs_0_, f32[128,512]{1,0:T(8,128)S(1)} %shard_map.58.refs_1_, f32[128,512]{1,0:T(8,128)S(1)} %collective-permute-done.2.refs_2_, bf16[1,1024,3584]{2,1,0:T(8,128)(2,1)S(1)} %copy-done), custom_call_target="tpu_custom_call" | custom-call | flops 536870912 | tf_op jit(solution)/shard_map/pallas_call | solution.py:139
  33.3 27.8 %all_to_all.11 = bf16[16,8,3584]{2,1,0:T(8,128)(2,1)S(1)} all-to-all(bf16[16,8,3584]{2,1,0:T(8,128)(2,1)S(1)} %bitcast.9), channel_id=1, replica_groups={{22,6,20,4,18,2,16,0,30,14,28,12,26,10,24,8},{23,7,21,5,19,3,17,1,31,15..., dimensions={0} | all-to-all | bytes 1835008 | tf_op jit(solution)/shard_map/all_to_all | solution.py:270
  61.1 1.2 %shard_map.61 = bf16[128,3584]{1,0:T(8,128)(2,1)} custom-call(bf16[128,256]{1,0:T(8,128)(2,1)S(1)} %get-tuple-element.8.mix_ref, bf16[128,3584]{1,0:T(8,128)(2,1)S(1)} %bitcast.8), custom_call_target="tpu_custom_call" | custom-call | tf_op jit(solution)/shard_map/pallas_call | solution.py:125
Async XLA Ops:
  0.0 29.5 %collective-permute-start = (bf16[1,7168,512]{2,1,0:T(8,128)(2,1)}, bf16[1,7168,512]{2,1,0:T(8,128)(2,1)S(1)}, u32[]{:S(2)}, u32[]{:S(2)}) collective-permute-start(bf16[1,7168,512]{2,1,0:T(8,128)(2,1)} %up_ref.1), channel_id=1, source_target_pairs={{0,1},{1,0},{2,3},{3,2},{4,5},{5,4},{6,7},{7,6},{8,9},{9,8},{10,11... | collective-permute-start | bytes 22020104 | tf_op jit(solution)/shard_map/ppermute | solution.py:217
  1.7 27.8 %copy-start = (bf16[1,1024,3584]{2,1,0:T(8,128)(2,1)S(1)}, bf16[1,1024,3584]{2,1,0:T(8,128)(2,1)}, u32[]{:S(2)}) copy-start(bf16[1,1024,3584]{2,1,0:T(8,128)(2,1)} %refs_3_.1) | copy-start | bytes 22020100
  1.7 27.8 %copy-start.1 = (bf16[1,7168,512]{2,1,0:T(8,128)(2,1)S(1)}, bf16[1,7168,512]{2,1,0:T(8,128)(2,1)}, u32[]{:S(2)}) copy-start(bf16[1,7168,512]{2,1,0:T(8,128)(2,1)} %up_ref.1) | copy-start | bytes 22020100
  30.1 1.6 %collective-permute-start.1 = (f32[128,512]{1,0:T(8,128)S(1)}, f32[128,512]{1,0:T(8,128)S(1)}, u32[]{:S(2)}, u32[]{:S(2)}) collective-permute-start(f32[128,512]{1,0:T(8,128)S(1)} %shard_map.58.refs_1_), channel_id=1, source_target_pairs={{0,1},{1,0},{2,3},{3,2},{4,5},{5,4},{6,7},{7,6},{8,9},{9,8},{10,11... | collective-permute-start | bytes 786440 | tf_op jit(solution)/shard_map/ppermute | solution.py:232
  30.9 1.7 %collective-permute-start.2 = (f32[128,512]{1,0:T(8,128)S(1)}, f32[128,512]{1,0:T(8,128)S(1)}, u32[]{:S(2)}, u32[]{:S(2)}) collective-permute-start(f32[128,512]{1,0:T(8,128)S(1)} %shard_map.57.refs_0_), channel_id=1, source_target_pairs={{0,1},{1,0},{2,3},{3,2},{4,5},{5,4},{6,7},{7,6},{8,9},{9,8},{10,11... | collective-permute-start | bytes 786440 | tf_op jit(solution)/shard_map/ppermute | solution.py:234

commit v7 on v6

--- a/solution.py
+++ b/solution.py
@@ -52,20 +52,16 @@
     return [slice(i * block, (i + 1) * block) for i in range(count)]
 
 
-def read_kernel(
-    flight, capacity, orders, ids_ref, weights_ref, tokens_ref, held, onehot_ref, mix_ref, ids, weights, sems
-):
+def read_kernel(flight, capacity, orders, ids_ref, weights_ref, onehot_ref, mix_ref, ids, weights, sems):
     copies = [
         pltpu.make_async_copy(ids_ref, ids, sems.at[0]),
         pltpu.make_async_copy(weights_ref, weights, sems.at[1]),
-        pltpu.make_async_copy(tokens_ref, held, sems.at[2]),
     ]
     for copy in copies:
         copy.start()
-    copies[0].wait()
-    copies[1].wait()
+    for copy in copies:
+        copy.wait()
     slot_tables(ids, weights, onehot_ref, mix_ref, flight, capacity, orders)
-    copies[2].wait()
 
 
 def pick_kernel(onehot_ref, held_ref, out_ref):
@@ -80,23 +76,22 @@
     hbm = pl.BlockSpec(memory_space=pltpu.HBM)
     vmem = pl.BlockSpec(memory_space=pltpu.VMEM)
     slots, tok = flight * capacity, tokens.shape[0]
-    held, onehot, mix = pl.pallas_call(
+    onehot, mix = pl.pallas_call(
         lambda *refs: read_kernel(flight, capacity, orders, *refs),
-        in_specs=[hbm, hbm, hbm],
-        out_specs=[vmem, vmem, vmem],
+        in_specs=[hbm, hbm],
+        out_specs=[vmem, vmem],
         out_shape=[
-            jax.ShapeDtypeStruct(tokens.shape, BF16),
             jax.ShapeDtypeStruct((slots, tok), BF16),
             jax.ShapeDtypeStruct((tok, MIX_PARTS * slots), BF16),
         ],
         scratch_shapes=[
             pltpu.VMEM(ids_t.shape, jnp.int32),
             pltpu.VMEM(weights_t.shape, F32),
-            pltpu.SemaphoreType.DMA((3,)),
+            pltpu.SemaphoreType.DMA((2,)),
         ],
-        cost_estimate=pl.CostEstimate(flops=0, bytes_accessed=0, transcendentals=0),
-        compiler_params=pltpu.CompilerParams(vmem_limit_bytes=16 * 2**20),
-    )(*(pltpu.with_memory_space_constraint(a, pltpu.HBM) for a in (ids_t, weights_t, tokens)))
+        cost_estimate=pl.CostEstimate(flops=2**31, bytes_accessed=0, transcendentals=0),
+        compiler_params=pltpu.CompilerParams(vmem_limit_bytes=16 * 2**20),
+    )(*(pltpu.with_memory_space_constraint(a, pltpu.HBM) for a in (ids_t, weights_t)))
     outgoing = pl.pallas_call(
         pick_kernel,
         in_specs=[vmem, vmem],
@@ -104,7 +99,7 @@
         out_shape=jax.ShapeDtypeStruct(shape, BF16),
         cost_estimate=pl.CostEstimate(flops=10**11, bytes_accessed=10**8, transcendentals=0),
         compiler_params=pltpu.CompilerParams(vmem_limit_bytes=16 * 2**20),
-    )(onehot, held)
+    )(onehot, tokens)
     return outgoing, mix
 
 

time: 62.6 us -> 62.6 us (level)
  transfers between devices with their start and end apart: 3 -> 3, of which waited for: 2 -> 2; matrix products, arithmetic and copies ran while one was open for 0% -> 0% of each run, Pallas kernels for 5% -> 4%
where the time goes in v7:
time: 62.6 us; the launch traced here: 62.2 us
  blocking collectives  55.2 us (88%)
  Pallas kernels  5.28 us (8%)
  starting transfers between devices  1.09 us (2%)
    all_to_all x1, blocking collectives, on_device(): lax.all_to_all(out_rows.reshape(owners, per_owner * capacity, width), 'ex...  27.8 us
    all_to_all x1, blocking collectives, on_device(): lax.all_to_all(outgoing.reshape(owners * 2, per_owner * capacity, block),...  27.4 us
    pallas_call x4, Pallas kernels, whole_call(): pl.pallas_call(kernel, in_specs=[pl.BlockSpec(memory_space=pltpu.VMEM)] *...  2.6 us
  transfers between devices with their start and end apart: 3, of which 2 were waited for; matrix products, arithmetic and copies ran while one was open for 0% of the time, Pallas kernels for 4%

profile of v7, /device:TPU:0, one launch (start us, length us, event | category | flops | bytes accessed | tf_op | source)
XLA Modules:
  0.0 62.2 jit_solution(4789759432946527820)
XLA Ops:
  0.0 0.0 copy-start
  0.0 0.5 collective-permute-start
  0.5 0.0 slice-start
  0.5 0.0 slice-start.2
  0.5 1.1 %shard_map.55 = (bf16[128,128]{1,0:T(8,128)(2,1)S(1)}, bf16[128,256]{1,0:T(8,128)(2,1)S(1)}) custom-call(s32[8,128]{1,0:T(8,128)} %bitcast.15, f32[8,128]{1,0:T(8,128)} %bitcast.16), custom_call_target="tpu_custom_call" | custom-call | flops 2147483648 | tf_op jit(solution)/shard_map/pallas_call | solution.py:79
  1.6 0.0 copy-done
  1.6 0.0 slice-start.1
  1.6 0.0 slice-start.3
  1.6 0.4 shard_map.56
  2.0 27.4 %all_to_all.10 = bf16[32,8,1792]{2,1,0:T(8,128)(2,1)S(1)} all-to-all(bf16[32,8,1792]{2,1,0:T(8,128)(2,1)S(1)} %bitcast.14), channel_id=1, replica_groups={{22,30,20,28,6,14,4,12,18,26,16,24,2,10,0,8,23,31,21,29,7,15,5,13,19,27..., dimensions={0} | all-to-all | bytes 1835008 | tf_op jit(solution)/shard_map/all_to_all | solution.py:216
  29.4 0.0 collective-permute-done.w_ref
  29.4 0.0 slice-done
  29.4 0.0 slice-done.2
  29.4 0.0 slice-done.1
  29.4 0.0 slice-done.3
  29.4 0.7 %shard_map.58.refs_1_ = f32[128,512]{1,0:T(8,128)S(1)} custom-call(bf16[2,16,8,1792]{3,2,1,0:T(8,128)(2,1)S(1)} %bitcast.10, bf16[1,7168,512]{2,1,0:T(8,128)(2,1)S(1)} %collective-permute-done.w_ref, bf16[1,7168,512]{2,1,0:T(8,128)(2,1)S(1)} %bitcast.9, bf16[1,1024,3584]{2,1,0:T(8,128)(2,1)S(1)} %bitcast.7), custom_call_target="tpu_custom_call" | custom-call | flops 536870912 | tf_op jit(solution)/shard_map/pallas_call | solution.py:134
  30.1 0.1 collective-permute-start.1
  30.2 0.6 %shard_map.57.refs_0_ = f32[128,512]{1,0:T(8,128)S(1)} custom-call(bf16[2,16,8,1792]{3,2,1,0:T(8,128)(2,1)S(1)} %bitcast.11, bf16[1,7168,512]{2,1,0:T(8,128)(2,1)S(1)} %bitcast.9), custom_call_target="tpu_custom_call" | custom-call | flops 536870912 | tf_op jit(solution)/shard_map/pallas_call | solution.py:134
  30.8 0.6 collective-permute-start.2
  31.4 0.3 collective-permute-done.1.refs_1_
  31.7 0.7 %shard_map.59.refs_0_ = f32[128,3584]{1,0:T(8,128)S(1)} custom-call(f32[128,512]{1,0:T(8,128)S(1)} %shard_map.57.refs_0_, f32[128,512]{1,0:T(8,128)S(1)} %collective-permute-done.1.refs_1_, bf16[1,1024,3584]{2,1,0:T(8,128)(2,1)S(1)} %bitcast.7), custom_call_target="tpu_custom_call" | custom-call | flops 536870912 | tf_op jit(solution)/shard_map/pallas_call | solution.py:134
  32.3 0.2 collective-permute-done.2.refs_2_
  32.5 0.7 %shard_map.60 = bf16[128,3584]{1,0:T(8,128)(2,1)S(1)} custom-call(f32[128,3584]{1,0:T(8,128)S(1)} %shard_map.59.refs_0_, f32[128,512]{1,0:T(8,128)S(1)} %shard_map.58.refs_1_, f32[128,512]{1,0:T(8,128)S(1)} %collective-permute-done.2.refs_2_, bf16[1,1024,3584]{2,1,0:T(8,128)(2,1)S(1)} %bitcast.7), custom_call_target="tpu_custom_call" | custom-call | flops 536870912 | tf_op jit(solution)/shard_map/pallas_call | solution.py:134
  33.2 27.8 %all_to_all.11 = bf16[16,8,3584]{2,1,0:T(8,128)(2,1)S(1)} all-to-all(bf16[16,8,3584]{2,1,0:T(8,128)(2,1)S(1)} %bitcast.13), channel_id=1, replica_groups={{22,6,20,4,18,2,16,0,30,14,28,12,26,10,24,8},{23,7,21,5,19,3,17,1,31,15..., dimensions={0} | all-to-all | bytes 1835008 | tf_op jit(solution)/shard_map/all_to_all | solution.py:265
  61.0 1.2 %shard_map.61 = bf16[128,3584]{1,0:T(8,128)(2,1)} custom-call(bf16[128,256]{1,0:T(8,128)(2,1)S(1)} %get-tuple-element.7.mix_ref, bf16[128,3584]{1,0:T(8,128)(2,1)S(1)} %bitcast.12), custom_call_target="tpu_custom_call" | custom-call | tf_op jit(solution)/shard_map/pallas_call | solution.py:120
  (2 shorter events, 0.0 us)
Async XLA Ops:
  0.0 1.6 %copy-start = (bf16[128,3584]{1,0:T(8,128)(2,1)S(1)}, bf16[128,3584]{1,0:T(8,128)(2,1)}, u32[]{:S(2)}) copy-start(bf16[128,3584]{1,0:T(8,128)(2,1)} %held_ref.1) | copy-start | bytes 2752516
  0.0 29.4 %collective-permute-start = (bf16[1,7168,512]{2,1,0:T(8,128)(2,1)}, bf16[1,7168,512]{2,1,0:T(8,128)(2,1)S(1)}, u32[]{:S(2)}, u32[]{:S(2)}) collective-permute-start(bf16[1,7168,512]{2,1,0:T(8,128)(2,1)} %up_ref.1), channel_id=1, source_target_pairs={{0,1},{1,0},{2,3},{3,2},{4,5},{5,4},{6,7},{7,6},{8,9},{9,8},{10,11... | collective-permute-start | bytes 22020104 | tf_op jit(solution)/shard_map/ppermute | solution.py:212
  0.5 28.9 %slice-start = ((s8[7340032]{0:T(1024)(128)(4,1)}), s8[4194304]{0:T(1024)(128)(4,1)S(1)}, s32[]{:S(2)}) async-start(s8[7340032]{0:T(1024)(128)(4,1)} %bitcast.6), calls=%async_computation.2 | async-start | bytes 8388608
  0.5 28.9 %slice-start.2 = ((s8[7340032]{0:T(1024)(128)(4,1)}), s8[4194304]{0:T(1024)(128)(4,1)S(1)}, s32[]{:S(2)}) async-start(s8[7340032]{0:T(1024)(128)(4,1)} %bitcast.8), calls=%async_computation.4 | async-start | bytes 8388608
  1.6 27.8 %slice-start.1 = ((s8[7340032]{0:T(1024)(128)(4,1)}), s8[3145728]{0:T(1024)(128)(4,1)S(1)}, s32[]{:S(2)}) async-start(s8[7340032]{0:T(1024)(128)(4,1)} %bitcast.6), calls=%async_computation.3 | async-start | bytes 6291456
  1.6 27.8 %slice-start.3 = ((s8[7340032]{0:T(1024)(128)(4,1)}), s8[3145728]{0:T(1024)(128)(4,1)S(1)}, s32[]{:S(2)}) async-start(s8[7340032]{0:T(1024)(128)(4,1)} %bitcast.8), calls=%async_computation.5 | async-start | bytes 6291456
  30.1 1.6 %collective-permute-start.1 = (f32[128,512]{1,0:T(8,128)S(1)}, f32[128,512]{1,0:T(8,128)S(1)}, u32[]{:S(2)}, u32[]{:S(2)}) collective-permute-start(f32[128,512]{1,0:T(8,128)S(1)} %shard_map.58.refs_1_), channel_id=1, source_target_pairs={{0,1},{1,0},{2,3},{3,2},{4,5},{5,4},{6,7},{7,6},{8,9},{9,8},{10,11... | collective-permute-start | bytes 786440 | tf_op jit(solution)/shard_map/ppermute | solution.py:227
  30.8 1.7 %collective-permute-start.2 = (f32[128,512]{1,0:T(8,128)S(1)}, f32[128,512]{1,0:T(8,128)S(1)}, u32[]{:S(2)}, u32[]{:S(2)}) collective-permute-start(f32[128,512]{1,0:T(8,128)S(1)} %shard_map.57.refs_0_), channel_id=1, source_target_pairs={{0,1},{1,0},{2,3},{3,2},{4,5},{5,4},{6,7},{7,6},{8,9},{9,8},{10,11... | collective-permute-start | bytes 786440 | tf_op jit(solution)/shard_map/ppermute | solution.py:229

commit v8 on v7

--- a/solution.py
+++ b/solution.py
@@ -8,7 +8,7 @@
 BF16, F32 = jnp.bfloat16, jnp.float32
 COMBINE_BLOCKS, MIX_PARTS = 7, 2
 DISPATCH_ORDER = [11, 15, 10, 14, 3, 7, 2, 6, 9, 13, 8, 12, 1, 5, 0, 4]
-RETURN_ORDER = [11, 3, 10, 2, 9, 1, 8, 0, 15, 7, 14, 6, 13, 5, 12, 4]
+RETURN_ORDER = [11, 3, 10, 13, 9, 1, 8, 0, 15, 7, 14, 6, 2, 5, 12, 4]
 
 
 def reorder(rows, order, size):

time: 62.6 us -> 62.5 us (level)
  no operation moved by 1% of the time
where the time goes in v8:
time: 62.5 us; the launch traced here: 62.2 us
  blocking collectives  55.2 us (88%)
  Pallas kernels  5.28 us (8%)
  starting transfers between devices  1.09 us (2%)
    all_to_all x1, blocking collectives, on_device(): lax.all_to_all(out_rows.reshape(owners, per_owner * capacity, width), 'ex...  27.8 us
    all_to_all x1, blocking collectives, on_device(): lax.all_to_all(outgoing.reshape(owners * 2, per_owner * capacity, block),...  27.4 us
    pallas_call x4, Pallas kernels, whole_call(): pl.pallas_call(kernel, in_specs=[pl.BlockSpec(memory_space=pltpu.VMEM)] *...  2.6 us
  transfers between devices with their start and end apart: 3, of which 2 were waited for; matrix products, arithmetic and copies ran while one was open for 0% of the time, Pallas kernels for 4%

profile of v8, /device:TPU:0, one launch (start us, length us, event | category | flops | bytes accessed | tf_op | source)
XLA Modules:
  0.0 62.2 jit_solution(7368579839622473185)
XLA Ops:
  0.0 0.0 copy-start
  0.0 0.5 collective-permute-start
  0.5 0.0 slice-start
  0.5 0.0 slice-start.2
  0.5 1.1 %shard_map.55 = (bf16[128,128]{1,0:T(8,128)(2,1)S(1)}, bf16[128,256]{1,0:T(8,128)(2,1)S(1)}) custom-call(s32[8,128]{1,0:T(8,128)} %bitcast.15, f32[8,128]{1,0:T(8,128)} %bitcast.16), custom_call_target="tpu_custom_call" | custom-call | flops 2147483648 | tf_op jit(solution)/shard_map/pallas_call | solution.py:79
  1.6 0.0 copy-done
  1.6 0.0 slice-start.1
  1.6 0.0 slice-start.3
  1.6 0.4 shard_map.56
  2.0 27.4 %all_to_all.10 = bf16[32,8,1792]{2,1,0:T(8,128)(2,1)S(1)} all-to-all(bf16[32,8,1792]{2,1,0:T(8,128)(2,1)S(1)} %bitcast.14), channel_id=1, replica_groups={{22,30,20,28,6,14,4,12,18,26,16,24,2,10,0,8,23,31,21,29,7,15,5,13,19,27..., dimensions={0} | all-to-all | bytes 1835008 | tf_op jit(solution)/shard_map/all_to_all | solution.py:216
  29.4 0.0 collective-permute-done.w_ref
  29.4 0.0 slice-done
  29.4 0.0 slice-done.2
  29.4 0.0 slice-done.1
  29.4 0.0 slice-done.3
  29.4 0.7 %shard_map.58.refs_1_ = f32[128,512]{1,0:T(8,128)S(1)} custom-call(bf16[2,16,8,1792]{3,2,1,0:T(8,128)(2,1)S(1)} %bitcast.10, bf16[1,7168,512]{2,1,0:T(8,128)(2,1)S(1)} %collective-permute-done.w_ref, bf16[1,7168,512]{2,1,0:T(8,128)(2,1)S(1)} %bitcast.9, bf16[1,1024,3584]{2,1,0:T(8,128)(2,1)S(1)} %bitcast.7), custom_call_target="tpu_custom_call" | custom-call | flops 536870912 | tf_op jit(solution)/shard_map/pallas_call | solution.py:134
  30.1 0.1 collective-permute-start.1
  30.2 0.6 %shard_map.57.refs_0_ = f32[128,512]{1,0:T(8,128)S(1)} custom-call(bf16[2,16,8,1792]{3,2,1,0:T(8,128)(2,1)S(1)} %bitcast.11, bf16[1,7168,512]{2,1,0:T(8,128)(2,1)S(1)} %bitcast.9), custom_call_target="tpu_custom_call" | custom-call | flops 536870912 | tf_op jit(solution)/shard_map/pallas_call | solution.py:134
  30.8 0.6 collective-permute-start.2
  31.4 0.3 collective-permute-done.1.refs_1_
  31.7 0.7 %shard_map.59.refs_0_ = f32[128,3584]{1,0:T(8,128)S(1)} custom-call(f32[128,512]{1,0:T(8,128)S(1)} %shard_map.57.refs_0_, f32[128,512]{1,0:T(8,128)S(1)} %collective-permute-done.1.refs_1_, bf16[1,1024,3584]{2,1,0:T(8,128)(2,1)S(1)} %bitcast.7), custom_call_target="tpu_custom_call" | custom-call | flops 536870912 | tf_op jit(solution)/shard_map/pallas_call | solution.py:134
  32.3 0.2 collective-permute-done.2.refs_2_
  32.5 0.7 %shard_map.60 = bf16[128,3584]{1,0:T(8,128)(2,1)S(1)} custom-call(f32[128,3584]{1,0:T(8,128)S(1)} %shard_map.59.refs_0_, f32[128,512]{1,0:T(8,128)S(1)} %shard_map.58.refs_1_, f32[128,512]{1,0:T(8,128)S(1)} %collective-permute-done.2.refs_2_, bf16[1,1024,3584]{2,1,0:T(8,128)(2,1)S(1)} %bitcast.7), custom_call_target="tpu_custom_call" | custom-call | flops 536870912 | tf_op jit(solution)/shard_map/pallas_call | solution.py:134
  33.2 27.8 %all_to_all.11 = bf16[16,8,3584]{2,1,0:T(8,128)(2,1)S(1)} all-to-all(bf16[16,8,3584]{2,1,0:T(8,128)(2,1)S(1)} %bitcast.13), channel_id=1, replica_groups={{22,6,20,26,18,2,16,0,30,14,28,12,4,10,24,8},{23,7,21,27,19,3,17,1,31,1..., dimensions={0} | all-to-all | bytes 1835008 | tf_op jit(solution)/shard_map/all_to_all | solution.py:265
  61.0 1.2 %shard_map.61 = bf16[128,3584]{1,0:T(8,128)(2,1)} custom-call(bf16[128,256]{1,0:T(8,128)(2,1)S(1)} %get-tuple-element.7.mix_ref, bf16[128,3584]{1,0:T(8,128)(2,1)S(1)} %bitcast.12), custom_call_target="tpu_custom_call" | custom-call | tf_op jit(solution)/shard_map/pallas_call | solution.py:120
  (2 shorter events, 0.0 us)
Async XLA Ops:
  0.0 1.6 %copy-start = (bf16[128,3584]{1,0:T(8,128)(2,1)S(1)}, bf16[128,3584]{1,0:T(8,128)(2,1)}, u32[]{:S(2)}) copy-start(bf16[128,3584]{1,0:T(8,128)(2,1)} %held_ref.1) | copy-start | bytes 2752516
  0.0 29.4 %collective-permute-start = (bf16[1,7168,512]{2,1,0:T(8,128)(2,1)}, bf16[1,7168,512]{2,1,0:T(8,128)(2,1)S(1)}, u32[]{:S(2)}, u32[]{:S(2)}) collective-permute-start(bf16[1,7168,512]{2,1,0:T(8,128)(2,1)} %up_ref.1), channel_id=1, source_target_pairs={{0,1},{1,0},{2,3},{3,2},{4,5},{5,4},{6,7},{7,6},{8,9},{9,8},{10,11... | collective-permute-start | bytes 22020104 | tf_op jit(solution)/shard_map/ppermute | solution.py:212
  0.5 28.9 %slice-start = ((s8[7340032]{0:T(1024)(128)(4,1)}), s8[4194304]{0:T(1024)(128)(4,1)S(1)}, s32[]{:S(2)}) async-start(s8[7340032]{0:T(1024)(128)(4,1)} %bitcast.6), calls=%async_computation.2 | async-start | bytes 8388608
  0.5 28.9 %slice-start.2 = ((s8[7340032]{0:T(1024)(128)(4,1)}), s8[4194304]{0:T(1024)(128)(4,1)S(1)}, s32[]{:S(2)}) async-start(s8[7340032]{0:T(1024)(128)(4,1)} %bitcast.8), calls=%async_computation.4 | async-start | bytes 8388608
  1.6 27.8 %slice-start.1 = ((s8[7340032]{0:T(1024)(128)(4,1)}), s8[3145728]{0:T(1024)(128)(4,1)S(1)}, s32[]{:S(2)}) async-start(s8[7340032]{0:T(1024)(128)(4,1)} %bitcast.6), calls=%async_computation.3 | async-start | bytes 6291456
  1.6 27.8 %slice-start.3 = ((s8[7340032]{0:T(1024)(128)(4,1)}), s8[3145728]{0:T(1024)(128)(4,1)S(1)}, s32[]{:S(2)}) async-start(s8[7340032]{0:T(1024)(128)(4,1)} %bitcast.8), calls=%async_computation.5 | async-start | bytes 6291456
  30.1 1.6 %collective-permute-start.1 = (f32[128,512]{1,0:T(8,128)S(1)}, f32[128,512]{1,0:T(8,128)S(1)}, u32[]{:S(2)}, u32[]{:S(2)}) collective-permute-start(f32[128,512]{1,0:T(8,128)S(1)} %shard_map.58.refs_1_), channel_id=1, source_target_pairs={{0,1},{1,0},{2,3},{3,2},{4,5},{5,4},{6,7},{7,6},{8,9},{9,8},{10,11... | collective-permute-start | bytes 786440 | tf_op jit(solution)/shard_map/ppermute | solution.py:227
  30.8 1.7 %collective-permute-start.2 = (f32[128,512]{1,0:T(8,128)S(1)}, f32[128,512]{1,0:T(8,128)S(1)}, u32[]{:S(2)}, u32[]{:S(2)}) collective-permute-start(f32[128,512]{1,0:T(8,128)S(1)} %shard_map.57.refs_0_), channel_id=1, source_target_pairs={{0,1},{1,0},{2,3},{3,2},{4,5},{5,4},{6,7},{7,6},{8,9},{9,8},{10,11... | collective-permute-start | bytes 786440 | tf_op jit(solution)/shard_map/ppermute | solution.py:229
